TPU v7x, 1024 devices: a whole 4x4x32 slice. The times are simulated.
1024 devices in a mesh: section: 8 (over z_lo), dp: 16 (over x, z_hi), tensor: 8 (over y, core).
Axes of the slice: x: 4, y: 4, z: 32 (z_hi: 4, z_lo: 8; z = z_hi * 8 + z_lo), core: 2. Of those that a mesh axis runs over, the one named last changes fastest.
Arguments:
- queries: bfloat16 [8, 4096, 8192], P('section', 'dp', 'tensor'), may hold values from -256 to 256
- image: bfloat16 [8192, 2048], P(('section', 'tensor'), 'dp'), may hold values from -6 to 6
- w_key: bfloat16 [8, 8192, 1024], P('section', None, 'tensor'), may hold values from -0.0625 to 0.0625
- w_value: bfloat16 [8, 8192, 1024], P('section', None, 'tensor'), may hold values from -0.0625 to 0.0625
- gates: float32 [8], P('section'), may hold values from 0.3 to 1.5
- tiles: int32 [16], P('dp'), may hold values from 1 to 4, as said below
- cotangent: bfloat16 [8, 4096, 8192], P('section', 'dp', 'tensor'), may hold values from -6 to 6
Outputs:
- attended: bfloat16 [8, 4096, 8192], P('section', 'dp', 'tensor')
- d_queries: bfloat16 [8, 4096, 8192], P('section', 'dp', 'tensor')
- d_image: bfloat16 [8192, 2048], P(('section', 'tensor'), 'dp')
Inputs may be any that keep to these rules, and one draw needn't show every extreme that they name: The first tiles[b] * 32 image tokens are valid for sample b; some sample has 4 tiles and some has one.
All inputs are finite; a program needn't handle non-finite values.
Results may differ from a plain program's by a relative error of at most 0.013.
The roundings to bfloat16 on the way count: a program that leaves them out, or rounds other values in their place, can miss the bound.
Values may be sent and summed in bfloat16 or wider, within the bound.
No kernel may reach another device: no remote copies, remote signals or barrier semaphores. Data moves between devices by JAX's collectives and lax.ppermute only.
A program may use at most 32 MiB of HBM per device.

v0:
```python
import functools
import math

import jax
import jax.numpy as jnp
from jax import lax
from jax.experimental import pallas as pl
from jax.experimental.pallas import tpu as pltpu
from jax.sharding import PartitionSpec as P


HD = 128
TILE_TOK = 32
IMG = 128
BLK = 128
N_SEC = 8
N_TEN = 8
N_HALF = 4
GROUP = 8
TXT = 256
VMEM_GRANT = 16 << 20
VMEM_GRANT = 16 << 20

F32 = jnp.float32
BF16 = jnp.bfloat16


NN = (((1,), (0,)), ((), ()))
NT = (((1,), (1,)), ((), ()))
TN = (((0,), (0,)), ((), ()))


def dot(a, b, dims):
    return lax.dot_general(a, b, dims, preferred_element_type=F32)


def slots(t):
    step = 2 - 4 * (((t >> 1) + t) & 1)
    return [t, (t + step) % N_TEN, (t - step) % N_TEN, (t + 4) % N_TEN]


def project(total, img_ref, own_ref, peer_ref, base):
    for n in range(2):
        for j in range(0, N_SEC, 2):
            left = jnp.concatenate([img_ref[n, j], img_ref[n, j + 1]], axis=1)
            right = jnp.concatenate(
                [ref[kv, base + n, j : j + 2].reshape(2 * BLK, HD) for ref in (own_ref, peer_ref) for kv in range(2)],
                axis=1,
            )
            part = dot(left, right, NN)
            total = part if total is None else total + part
    return total


def near_kernel(img_ref, own_ref, peer_ref, out_ref):
    out_ref[...] = project(None, img_ref, own_ref, peer_ref, 0)


def far_kernel(part_ref, img_ref, own_ref, peer_ref, out_ref, send_ref):
    total = project(part_ref[...], img_ref, own_ref, peer_ref, 2)
    out_ref[...] = total[:, : 2 * HD]
    send_ref[...] = total[:, 2 * HD :]


def term(own_ref, peer_ref, grads, slot):
    weights = jnp.concatenate(
        [ref[kv, slot].reshape(N_SEC * BLK, HD) for ref in (own_ref, peer_ref) for kv in range(2)], axis=1
    )
    return dot(weights, grads, NT).reshape(N_SEC, BLK, IMG)


def term_kernel(slot, own_ref, peer_ref, grads_ref, others_ref, out_ref):
    grads = jnp.concatenate([grads_ref[...], others_ref[...]], axis=1)
    out_ref[...] = term(own_ref, peer_ref, grads, slot).astype(out_ref.dtype)


def attention_kernel(
    tiles_ref, gate_ref, part_ref, got_ref, q_ref, up_ref, probs_ref, dscores_ref, rows_ref, grads_ref
):
    rows = (part_ref[...] + got_ref[...]).astype(BF16)
    rows_ref[...] = rows
    keys = rows[:, :HD]
    values = rows[:, HD:]
    scale = jnp.tanh(jnp.full((1, HD), gate_ref[0], F32))
    limit = tiles_ref[0] * TILE_TOK
    allowed = lax.broadcasted_iota(jnp.int32, (IMG, TXT), 0) < limit
    d_keys = d_values = None
    for h in range(GROUP):
        query = q_ref[:, h * HD : (h + 1) * HD]
        upstream = up_ref[:, h * HD : (h + 1) * HD].astype(F32)
        d_context = (scale * upstream).astype(BF16)
        scores = dot(keys, query, NT) * F32(1.0 / math.sqrt(HD))
        scores = jnp.where(allowed, scores, F32(-1e30))
        top = jnp.max(scores, axis=0, keepdims=True)
        expo = jnp.exp(scores - top)
        probs = expo * (1.0 / jnp.sum(expo, axis=0, keepdims=True))
        probs_b = probs.astype(BF16)
        probs_ref[h] = probs_b
        d_probs = dot(values, d_context, NT)
        delta = jnp.sum(probs * d_probs, axis=0, keepdims=True)
        d_scores = (probs * (d_probs - delta) * F32(1.0 / math.sqrt(HD))).astype(BF16)
        dscores_ref[h] = d_scores
        dv = dot(probs_b, d_context, NN)
        dk = dot(d_scores, query, NN)
        d_values = dv if d_values is None else d_values + dv
        d_keys = dk if d_keys is None else d_keys + dk
    grads = jnp.concatenate([d_keys.astype(BF16), d_values.astype(BF16)], axis=1)
    grads_ref[...] = grads


def join_kernel(keep_ref, a_ref, b_ref, c_ref, out_ref):
    total = keep_ref[...] + a_ref[...].astype(F32)
    out_ref[...] = (total + b_ref[...].astype(F32) + c_ref[...].astype(F32)).astype(BF16)


def attended_kernel(gate_ref, probs_ref, rows_ref, out_ref):
    values = rows_ref[:, HD:]
    scale = jnp.tanh(jnp.full((1, HD), gate_ref[0], F32))
    for h in range(GROUP):
        context = dot(probs_ref[h], values, TN)
        out_ref[:, h * HD : (h + 1) * HD] = (scale * context).astype(BF16)


def dquery_kernel(dscores_ref, rows_ref, out_ref):
    keys = rows_ref[:, :HD]
    for h in range(GROUP):
        out_ref[:, h * HD : (h + 1) * HD] = dot(dscores_ref[h], keys, TN).astype(BF16)


def arr(dtype, *shape):
    return pltpu.VMEM(shape, dtype)


SMEM_SPEC = pl.BlockSpec(memory_space=pltpu.SMEM)
VMEM_SPEC = pl.BlockSpec(memory_space=pltpu.VMEM)


def call(kernel, outs, flops, *args):
    return pl.pallas_call(
        kernel,
        out_shape=outs,
        in_specs=[SMEM_SPEC if a.ndim == 1 else VMEM_SPEC for a in args],
        out_specs=jax.tree.map(lambda _: VMEM_SPEC, outs),
        cost_estimate=pl.CostEstimate(flops=flops, transcendentals=0, bytes_accessed=1 << 20),
        compiler_params=pltpu.CompilerParams(vmem_limit_bytes=VMEM_GRANT),
    )(*[a if a.ndim == 1 else pltpu.with_memory_space_constraint(a, pltpu.VMEM) for a in args])


def outside(kernel, *args):
    return pl.pallas_call(
        kernel,
        out_shape=jax.ShapeDtypeStruct((TXT, GROUP * HD), BF16),
        in_specs=[SMEM_SPEC if a.ndim == 1 else VMEM_SPEC for a in args],
        out_specs=VMEM_SPEC,
        cost_estimate=pl.CostEstimate(flops=1 << 27, transcendentals=0, bytes_accessed=1 << 20),
        compiler_params=pltpu.CompilerParams(vmem_limit_bytes=VMEM_GRANT),
    )(*[a if a.ndim == 1 else pltpu.with_memory_space_constraint(a, pltpu.VMEM) for a in args])


def run(copies):
    for copy in copies:
        copy.start()
    for copy in copies:
        copy.wait()


def give_kernel(t_ref, wk_ref, wv_ref, out_ref, sem):
    picks = slots(t_ref[0] ^ 1)
    run([
        pltpu.make_async_copy(ref.at[:, pick], out_ref.at[kv, n], sem.at[kv, n])
        for kv, ref in enumerate((wk_ref, wv_ref))
        for n, pick in enumerate(picks)
    ])


def load_kernel(t_ref, wk_ref, wv_ref, q_ref, up_ref, out_ref, q_out, up_out, sem, q_sem, up_sem):
    picks = slots(t_ref[0])
    run([
        pltpu.make_async_copy(ref.at[:, pick], out_ref.at[kv, n], sem.at[kv, n])
        for kv, ref in enumerate((wk_ref, wv_ref))
        for n, pick in enumerate(picks)
    ] + [pltpu.make_async_copy(q_ref, q_out, q_sem), pltpu.make_async_copy(up_ref, up_out, up_sem)])


def load(kernel, outs, sems, place, *args):
    return pl.pallas_call(
        kernel,
        out_shape=outs,
        in_specs=[SMEM_SPEC] + [pl.BlockSpec(memory_space=pltpu.HBM) for _ in args],
        out_specs=jax.tree.map(lambda _: VMEM_SPEC, outs),
        scratch_shapes=sems,
        cost_estimate=pl.CostEstimate(flops=0, transcendentals=0, bytes_accessed=6 << 20),
        compiler_params=pltpu.CompilerParams(vmem_limit_bytes=VMEM_GRANT),
    )(place, *[pltpu.with_memory_space_constraint(a, pltpu.HBM) for a in args])


def shards(queries, image, w_key, w_value, gates, tiles, cotangent):
    wk = w_key.reshape(N_SEC, N_TEN, BLK, HD)
    wv = w_value.reshape(N_SEC, N_TEN, BLK, HD)
    text = queries[0]
    upstream = cotangent[0]
    me = lax.axis_index("tensor").astype(jnp.int32).reshape(1)

    def turn(t):
        return 2 - 4 * (((t >> 1) + t) & 1)

    partner = [(t, t ^ 1) for t in range(N_TEN)]
    first = [(t, (t + turn(t)) % N_TEN) for t in range(N_TEN)]
    second = [(t, (t - turn(t)) % N_TEN) for t in range(N_TEN)]

    def send(x, perm):
        return lax.ppermute(x, "tensor", perm)

    dma = pltpu.SemaphoreType.DMA
    half = arr(BF16, 2, N_HALF, N_SEC, BLK, HD)

    image, me, gates, tiles = lax.optimization_barrier((image, me, gates, tiles))
    flat = jnp.broadcast_to(image.T[None], (N_SEC, IMG, BLK))
    mine = lax.all_to_all(flat, "section", 0, 0)
    wk, wv, text, upstream, mine = lax.optimization_barrier((wk, wv, text, upstream, mine))
    got = send(mine, first)
    give = load(give_kernel, half, [dma((2, N_HALF))], me, wk, wv)
    peer = send(give, partner)
    got, give = lax.optimization_barrier((got, give))
    near = jnp.stack([mine, got])
    wk, wv, text, upstream, near = lax.optimization_barrier((wk, wv, text, upstream, near))
    far = send(near, second)
    own, text, upstream = load(
        load_kernel, (half, arr(BF16, *text.shape), arr(BF16, *upstream.shape)),
        [dma((2, N_HALF)), dma, dma], me, wk, wv, text, upstream,
    )
    part = call(near_kernel, arr(F32, IMG, 4 * HD), 1 << 29, near, own, peer)
    far, part = lax.optimization_barrier((far, part))
    part, out_part = call(far_kernel, (arr(F32, IMG, 2 * HD),) * 2, 1 << 29, part, far, own, peer)
    got_part = send(out_part, partner)

    probs, d_scores, rows, grads = call(
        attention_kernel,
        (arr(BF16, GROUP, IMG, TXT), arr(BF16, GROUP, IMG, TXT), arr(BF16, IMG, 2 * HD), arr(BF16, IMG, 2 * HD)),
        1 << 30, tiles, gates, part, got_part, text, upstream,
    )
    others = send(grads, partner)

    def terms(slot, dtype):
        return call(
            functools.partial(term_kernel, slot), arr(dtype, N_SEC, BLK, IMG), 1 << 28, own, peer, grads, others
        )

    opposite = [(t, (t + 4) % N_TEN) for t in range(N_TEN)]
    got_opposite = send(terms(3, BF16), opposite)
    got_first = send(terms(1, BF16), first)
    got_second = send(terms(2, BF16), second)
    keep = terms(0, F32)
    attended = outside(attended_kernel, gates, probs, rows)
    d_query = outside(dquery_kernel, d_scores, rows)
    keep, attended, d_query = lax.optimization_barrier((keep, attended, d_query))
    total = call(join_kernel, arr(BF16, N_SEC, BLK, IMG), 1 << 20, keep, got_opposite, got_first, got_second)
    pieces = lax.all_to_all(total, "section", 0, 0)
    grad = jnp.sum(pieces.astype(F32), axis=0).astype(BF16)
    return (attended[None], d_query[None], grad)


def solution(mesh):
    return jax.shard_map(
        shards,
        mesh=mesh,
        in_specs=(
            P("section", "dp", "tensor"),
            P(("section", "tensor"), "dp"),
            P("section", None, "tensor"),
            P("section", None, "tensor"),
            P("section"),
            P("dp"),
            P("section", "dp", "tensor"),
        ),
        out_specs=(
            P("section", "dp", "tensor"),
            P("section", "dp", "tensor"),
            P(("section", "tensor"), "dp"),
        ),
        check_vma=False,
    )
```

profile of v0, /device:TPU:6, one launch (start us, length us, event | category | flops | bytes accessed | tf_op | source)
XLA Modules:
  0.0 104.6 jit_solution(14270627394170631302)
XLA Ops:
  0.6 0.9 copy.10
  1.6 29.0 %all_to_all.10 = bf16[8,128,128]{2,1,0:T(8,128)(2,1)S(1)} all-to-all(bf16[8,128,128]{2,1,0:T(8,128)(2,1)S(1)} %broadcast_in_dim.12), channel_id=1, replica_groups=mesh['section'=8,'dp'=16,'tensor'=8] {'section'}, dimensions={0} | all-to-all | bytes 524288 | tf_op jit(solution)/shard_map/all_to_all | solution.py:219
  30.6 1.6 %shard_map.94 = bf16[2,4,8,128,128]{4,3,2,1,0:T(8,128)(2,1)S(1)} custom-call(s32[1]{0:T(128)} %bitcast.t_ref, bf16[8,8,128,128]{3,2,1,0:T(8,128)(2,1)} %bitcast.10, bf16[8,8,128,128]{3,2,1,0:T(8,128)(2,1)} %bitcast.12), custom_call_target="tpu_custom_call" | custom-call | bytes 6291456 | tf_op jit(solution)/shard_map/pallas_call | solution.py:186
  32.1 1.9 %collective-permute-start.1 = (bf16[2,4,8,128,128]{4,3,2,1,0:T(8,128)(2,1)S(1)}, bf16[2,4,8,128,128]{4,3,2,1,0:T(8,128)(2,1)S(1)}, u32[]{:S(2)}, u32[]{:S(2)}) collective-permute-start(bf16[2,4,8,128,128]{4,3,2,1,0:T(8,128)(2,1)S(1)} %shard_map.94), channel_id=1, source_target_pairs={{0,1},{1,0},{2,3},{3,2},{4,5},{5,4},{6,7},{7,6},{8,9},{9,8},{10,11... | collective-permute-start | bytes 6291464 | tf_op jit(solution)/shard_map/ppermute | solution.py:212
  34.1 3.5 %collective-permute-start = (bf16[8,128,128]{2,1,0:T(8,128)(2,1)S(1)}, bf16[8,128,128]{2,1,0:T(8,128)(2,1)S(1)}, u32[]{:S(2)}, u32[]{:S(2)}) collective-permute-start(bf16[8,128,128]{2,1,0:T(8,128)(2,1)S(1)} %all_to_all.10), channel_id=1, source_target_pairs={{0,2},{1,7},{2,0},{3,5},{4,6},{5,3},{6,4},{7,1},{8,10},{9,15},{10,... | collective-permute-start | bytes 786440 | tf_op jit(solution)/shard_map/ppermute | solution.py:212
  37.6 4.8 %collective-permute-done = bf16[8,128,128]{2,1,0:T(8,128)(2,1)S(1)} collective-permute-done((bf16[8,128,128]{2,1,0:T(8,128)(2,1)S(1)}, bf16[8,128,128]{2,1,0:T(8,128)(2,1)S(1)}, u32[]{:S(2)}, u32[]{:S(2)}) %collective-permute-start) | collective-permute-done | bytes 262176 | tf_op jit(solution)/shard_map/ppermute | solution.py:212
  42.3 0.1 pad_maximum_fusion.img_ref
  42.4 4.9 %collective-permute-start.2 = (bf16[2,8,128,128]{3,2,1,0:T(8,128)(2,1)S(1)}, bf16[2,8,128,128]{3,2,1,0:T(8,128)(2,1)S(1)}, u32[]{:S(2)}, u32[]{:S(2)}) collective-permute-start(bf16[2,8,128,128]{3,2,1,0:T(8,128)(2,1)S(1)} %pad_maximum_fusion.img_ref), channel_id=1, source_target_pairs={{0,6},{1,3},{2,4},{3,1},{4,2},{5,7},{6,0},{7,5},{8,14},{9,11},{10,... | collective-permute-start | bytes 1572872 | tf_op jit(solution)/shard_map/ppermute | solution.py:212
  47.3 1.9 %shard_map.95 = (bf16[2,4,8,128,128]{4,3,2,1,0:T(8,128)(2,1)S(1)}, bf16[256,1024]{1,0:T(8,128)(2,1)S(1)}, bf16[256,1024]{1,0:T(8,128)(2,1)S(1)}) custom-call(s32[1]{0:T(128)} %bitcast.t_ref, bf16[8,8,128,128]{3,2,1,0:T(8,128)(2,1)} %bitcast.11, bf16[8,8,128,128]{3,2,1,0:T(8,128)(2,1)} %bitcast.13, bf16[256,1024]{1,0:T(8,128)(2,1)} %bitcast.17, ...), custom_call_target="tpu_custom_call" | custom-call | bytes 6291456 | tf_op jit(solution)/shard_map/pallas_call | solution.py:186
  49.3 0.0 collective-permute-done.1.peer_ref
  49.3 0.5 shard_map.96.part_ref
  49.7 4.9 %collective-permute-done.2.img_ref = bf16[2,8,128,128]{3,2,1,0:T(8,128)(2,1)S(1)} collective-permute-done((bf16[2,8,128,128]{3,2,1,0:T(8,128)(2,1)S(1)}, bf16[2,8,128,128]{3,2,1,0:T(8,128)(2,1)S(1)}, u32[]{:S(2)}, u32[]{:S(2)}) %collective-permute-start.2) | collective-permute-done | bytes 524320 | tf_op jit(solution)/shard_map/ppermute | solution.py:212
  54.7 0.4 shard_map.97
  55.1 1.9 %collective-permute-start.3 = (f32[128,256]{1,0:T(8,128)S(1)}, f32[128,256]{1,0:T(8,128)S(1)}, u32[]{:S(2)}, u32[]{:S(2)}) collective-permute-start(f32[128,256]{1,0:T(8,128)S(1)} %get-tuple-element.51), channel_id=1, source_target_pairs={{0,1},{1,0},{2,3},{3,2},{4,5},{5,4},{6,7},{7,6},{8,9},{9,8},{10,11... | collective-permute-start | bytes 393224 | tf_op jit(solution)/shard_map/ppermute | solution.py:212
  58.3 0.0 collective-permute-done.3.got_ref
  58.4 2.0 %shard_map.98 = (bf16[8,128,256]{2,1,0:T(8,128)(2,1)S(1)}, bf16[8,128,256]{2,1,0:T(8,128)(2,1)S(1)}, bf16[128,256]{1,0:T(8,128)(2,1)S(1)}, bf16[128,256]{1,0:T(8,128)(2,1)S(1)}) custom-call(s32[1]{0:T(128)S(6)} %copy.12.tiles_ref, f32[1]{0:T(128)S(6)} %copy.11.gate_ref, f32[128,256]{1,0:T(8,128)S(1)} %get-tuple-element.50.part_ref, ...), custom_call_target="tpu_custom_call" | custom-call | flops 1073741824 | bytes 1048576 | tf_op jit(solution)/shard_map/pallas_call | solution.py:139
  60.4 2.4 %collective-permute-start.4 = (bf16[128,256]{1,0:T(8,128)(2,1)S(1)}, bf16[128,256]{1,0:T(8,128)(2,1)S(1)}, u32[]{:S(2)}, u32[]{:S(2)}) collective-permute-start(bf16[128,256]{1,0:T(8,128)(2,1)S(1)} %get-tuple-element.54.grads_ref), channel_id=1, source_target_pairs={{0,1},{1,0},{2,3},{3,2},{4,5},{5,4},{6,7},{7,6},{8,9},{9,8},{10,11... | collective-permute-start | bytes 196616 | tf_op jit(solution)/shard_map/ppermute | solution.py:212
  62.8 0.9 collective-permute-done.4.others_ref
  63.7 0.4 shard_map.102
  64.1 3.9 %collective-permute-start.5 = (bf16[8,128,128]{2,1,0:T(8,128)(2,1)S(1)}, bf16[8,128,128]{2,1,0:T(8,128)(2,1)S(1)}, u32[]{:S(2)}, u32[]{:S(2)}) collective-permute-start(bf16[8,128,128]{2,1,0:T(8,128)(2,1)S(1)} %shard_map.102), channel_id=1, source_target_pairs={{0,4},{1,5},{2,6},{3,7},{4,0},{5,1},{6,2},{7,3},{8,12},{9,13},{10,... | collective-permute-start | bytes 786440 | tf_op jit(solution)/shard_map/ppermute | solution.py:212
  68.0 0.4 shard_map.103
  68.5 3.8 %collective-permute-start.6 = (bf16[8,128,128]{2,1,0:T(8,128)(2,1)S(1)}, bf16[8,128,128]{2,1,0:T(8,128)(2,1)S(1)}, u32[]{:S(2)}, u32[]{:S(2)}) collective-permute-start(bf16[8,128,128]{2,1,0:T(8,128)(2,1)S(1)} %shard_map.103), channel_id=1, source_target_pairs={{0,2},{1,7},{2,0},{3,5},{4,6},{5,3},{6,4},{7,1},{8,10},{9,15},{10,... | collective-permute-start | bytes 786440 | tf_op jit(solution)/shard_map/ppermute | solution.py:212
  72.3 0.4 shard_map.104
  72.7 2.1 %collective-permute-start.7 = (bf16[8,128,128]{2,1,0:T(8,128)(2,1)S(1)}, bf16[8,128,128]{2,1,0:T(8,128)(2,1)S(1)}, u32[]{:S(2)}, u32[]{:S(2)}) collective-permute-start(bf16[8,128,128]{2,1,0:T(8,128)(2,1)S(1)} %shard_map.104), channel_id=1, source_target_pairs={{0,6},{1,3},{2,4},{3,1},{4,2},{5,7},{6,0},{7,5},{8,14},{9,11},{10,... | collective-permute-start | bytes 786440 | tf_op jit(solution)/shard_map/ppermute | solution.py:212
  74.8 1.1 %shard_map.100 = bf16[256,1024]{1,0:T(8,128)(2,1)} custom-call(f32[1]{0:T(128)S(6)} %copy.11.gate_ref, bf16[8,128,256]{2,1,0:T(8,128)(2,1)S(1)} %get-tuple-element.55.probs_ref, bf16[128,256]{1,0:T(8,128)(2,1)S(1)} %get-tuple-element.56.rows_ref), custom_call_target="tpu_custom_call" | custom-call | flops 134217728 | bytes 1048576 | tf_op jit(solution)/shard_map/pallas_call | solution.py:150
  76.0 1.1 %shard_map.101 = bf16[256,1024]{1,0:T(8,128)(2,1)} custom-call(bf16[8,128,256]{2,1,0:T(8,128)(2,1)S(1)} %get-tuple-element.57.dscores_ref, bf16[128,256]{1,0:T(8,128)(2,1)S(1)} %get-tuple-element.56.rows_ref), custom_call_target="tpu_custom_call" | custom-call | flops 134217728 | bytes 1048576 | tf_op jit(solution)/shard_map/pallas_call | solution.py:150
  77.1 0.4 shard_map.99.keep_ref
  77.5 4.5 %collective-permute-done.6.b_ref = bf16[8,128,128]{2,1,0:T(8,128)(2,1)S(1)} collective-permute-done((bf16[8,128,128]{2,1,0:T(8,128)(2,1)S(1)}, bf16[8,128,128]{2,1,0:T(8,128)(2,1)S(1)}, u32[]{:S(2)}, u32[]{:S(2)}) %collective-permute-start.6) | collective-permute-done | bytes 262176 | tf_op jit(solution)/shard_map/ppermute | solution.py:212
  82.1 0.1 collective-permute-done.7.c_ref
  82.2 0.1 shard_map.105
  82.3 21.6 %all_to_all.11 = bf16[8,128,128]{2,1,0:T(8,128)(2,1)S(1)} all-to-all(bf16[8,128,128]{2,1,0:T(8,128)(2,1)S(1)} %shard_map.105), channel_id=1, replica_groups=mesh['section'=8,'dp'=16,'tensor'=8] {'section'}, dimensions={0} | all-to-all | bytes 524288 | tf_op jit(solution)/shard_map/all_to_all | solution.py:258
  103.9 0.7 reduce_sum.12
  (2 shorter events, 0.0 us)
Async XLA Ops:
  32.1 17.1 %collective-permute-start.1 = (bf16[2,4,8,128,128]{4,3,2,1,0:T(8,128)(2,1)S(1)}, bf16[2,4,8,128,128]{4,3,2,1,0:T(8,128)(2,1)S(1)}, u32[]{:S(2)}, u32[]{:S(2)}) collective-permute-start(bf16[2,4,8,128,128]{4,3,2,1,0:T(8,128)(2,1)S(1)} %shard_map.94), channel_id=1, source_target_pairs={{0,1},{1,0},{2,3},{3,2},{4,5},{5,4},{6,7},{7,6},{8,9},{9,8},{10,11... | collective-permute-start | bytes 6291464 | tf_op jit(solution)/shard_map/ppermute | solution.py:212
  34.1 8.3 %collective-permute-start = (bf16[8,128,128]{2,1,0:T(8,128)(2,1)S(1)}, bf16[8,128,128]{2,1,0:T(8,128)(2,1)S(1)}, u32[]{:S(2)}, u32[]{:S(2)}) collective-permute-start(bf16[8,128,128]{2,1,0:T(8,128)(2,1)S(1)} %all_to_all.10), channel_id=1, source_target_pairs={{0,2},{1,7},{2,0},{3,5},{4,6},{5,3},{6,4},{7,1},{8,10},{9,15},{10,... | collective-permute-start | bytes 786440 | tf_op jit(solution)/shard_map/ppermute | solution.py:212
  42.4 12.3 %collective-permute-start.2 = (bf16[2,8,128,128]{3,2,1,0:T(8,128)(2,1)S(1)}, bf16[2,8,128,128]{3,2,1,0:T(8,128)(2,1)S(1)}, u32[]{:S(2)}, u32[]{:S(2)}) collective-permute-start(bf16[2,8,128,128]{3,2,1,0:T(8,128)(2,1)S(1)} %pad_maximum_fusion.img_ref), channel_id=1, source_target_pairs={{0,6},{1,3},{2,4},{3,1},{4,2},{5,7},{6,0},{7,5},{8,14},{9,11},{10,... | collective-permute-start | bytes 1572872 | tf_op jit(solution)/shard_map/ppermute | solution.py:212
  55.1 3.2 %collective-permute-start.3 = (f32[128,256]{1,0:T(8,128)S(1)}, f32[128,256]{1,0:T(8,128)S(1)}, u32[]{:S(2)}, u32[]{:S(2)}) collective-permute-start(f32[128,256]{1,0:T(8,128)S(1)} %get-tuple-element.51), channel_id=1, source_target_pairs={{0,1},{1,0},{2,3},{3,2},{4,5},{5,4},{6,7},{7,6},{8,9},{9,8},{10,11... | collective-permute-start | bytes 393224 | tf_op jit(solution)/shard_map/ppermute | solution.py:212
  60.4 3.3 %collective-permute-start.4 = (bf16[128,256]{1,0:T(8,128)(2,1)S(1)}, bf16[128,256]{1,0:T(8,128)(2,1)S(1)}, u32[]{:S(2)}, u32[]{:S(2)}) collective-permute-start(bf16[128,256]{1,0:T(8,128)(2,1)S(1)} %get-tuple-element.54.grads_ref), channel_id=1, source_target_pairs={{0,1},{1,0},{2,3},{3,2},{4,5},{5,4},{6,7},{7,6},{8,9},{9,8},{10,11... | collective-permute-start | bytes 196616 | tf_op jit(solution)/shard_map/ppermute | solution.py:212
  64.1 13.4 %collective-permute-start.5 = (bf16[8,128,128]{2,1,0:T(8,128)(2,1)S(1)}, bf16[8,128,128]{2,1,0:T(8,128)(2,1)S(1)}, u32[]{:S(2)}, u32[]{:S(2)}) collective-permute-start(bf16[8,128,128]{2,1,0:T(8,128)(2,1)S(1)} %shard_map.102), channel_id=1, source_target_pairs={{0,4},{1,5},{2,6},{3,7},{4,0},{5,1},{6,2},{7,3},{8,12},{9,13},{10,... | collective-permute-start | bytes 786440 | tf_op jit(solution)/shard_map/ppermute | solution.py:212
  68.5 13.6 %collective-permute-start.6 = (bf16[8,128,128]{2,1,0:T(8,128)(2,1)S(1)}, bf16[8,128,128]{2,1,0:T(8,128)(2,1)S(1)}, u32[]{:S(2)}, u32[]{:S(2)}) collective-permute-start(bf16[8,128,128]{2,1,0:T(8,128)(2,1)S(1)} %shard_map.103), channel_id=1, source_target_pairs={{0,2},{1,7},{2,0},{3,5},{4,6},{5,3},{6,4},{7,1},{8,10},{9,15},{10,... | collective-permute-start | bytes 786440 | tf_op jit(solution)/shard_map/ppermute | solution.py:212
  72.7 9.5 %collective-permute-start.7 = (bf16[8,128,128]{2,1,0:T(8,128)(2,1)S(1)}, bf16[8,128,128]{2,1,0:T(8,128)(2,1)S(1)}, u32[]{:S(2)}, u32[]{:S(2)}) collective-permute-start(bf16[8,128,128]{2,1,0:T(8,128)(2,1)S(1)} %shard_map.104), channel_id=1, source_target_pairs={{0,6},{1,3},{2,4},{3,1},{4,2},{5,7},{6,0},{7,5},{8,14},{9,11},{10,... | collective-permute-start | bytes 786440 | tf_op jit(solution)/shard_map/ppermute | solution.py:212
where the time goes:
time: 105 us
  blocking collectives  50.7 us (48%)
  starting transfers between devices  24.5 us (23%)
  waiting for transfers between devices  15.3 us (15%)
  Pallas kernels  10.5 us (10%)
  between operations  2.09 us (2%)
    all_to_all x1, blocking collectives, shards(): mine = lax.all_to_all(flat, 'section', 0, 0)  29 us
    ppermute x8, starting transfers between devices, send(): return lax.ppermute(x, 'tensor', perm)  24.5 us
    all_to_all x1, blocking collectives, shards(): pieces = lax.all_to_all(total, 'section', 0, 0)  21.6 us
    ppermute x8, waiting for transfers between devices, send(): return lax.ppermute(x, 'tensor', perm)  15.3 us
    pallas_call x8, Pallas kernels, call(): pl.pallas_call(kernel, out_shape=outs, in_specs=[SMEM_SPEC if a.ndim == 1...  4.76 us
    pallas_call x2, Pallas kernels, load(): pl.pallas_call(kernel, out_shape=outs, in_specs=[SMEM_SPEC] + [pl.BlockSp...  3.51 us
    pallas_call x2, Pallas kernels, outside(): pl.pallas_call(kernel, out_shape=jax.ShapeDtypeStruct((TXT, GROUP * HD),...  2.26 us
  transfers between devices with their start and end apart: 8, of which 5 were waited for; matrix products, arithmetic and copies ran while one was open for 0% of the time, Pallas kernels for 6%

commit v1 on v0

--- a/solution.py
+++ b/solution.py
@@ -39,25 +39,17 @@
     return [t, (t + step) % N_TEN, (t - step) % N_TEN, (t + 4) % N_TEN]
 
 
-def project(total, img_ref, own_ref, peer_ref, base):
-    for n in range(2):
+def project_kernel(a_ref, b_ref, c_ref, d_ref, own_ref, peer_ref, out_ref, send_ref):
+    total = None
+    for slot, img_ref in enumerate((a_ref, b_ref, c_ref, d_ref)):
         for j in range(0, N_SEC, 2):
-            left = jnp.concatenate([img_ref[n, j], img_ref[n, j + 1]], axis=1)
+            left = jnp.concatenate([img_ref[j], img_ref[j + 1]], axis=1)
             right = jnp.concatenate(
-                [ref[kv, base + n, j : j + 2].reshape(2 * BLK, HD) for ref in (own_ref, peer_ref) for kv in range(2)],
+                [ref[kv, slot, j : j + 2].reshape(2 * BLK, HD) for ref in (own_ref, peer_ref) for kv in range(2)],
                 axis=1,
             )
             part = dot(left, right, NN)
             total = part if total is None else total + part
-    return total
-
-
-def near_kernel(img_ref, own_ref, peer_ref, out_ref):
-    out_ref[...] = project(None, img_ref, own_ref, peer_ref, 0)
-
-
-def far_kernel(part_ref, img_ref, own_ref, peer_ref, out_ref, send_ref):
-    total = project(part_ref[...], img_ref, own_ref, peer_ref, 2)
     out_ref[...] = total[:, : 2 * HD]
     send_ref[...] = total[:, 2 * HD :]
 
@@ -206,6 +198,7 @@
 
     partner = [(t, t ^ 1) for t in range(N_TEN)]
     first = [(t, (t + turn(t)) % N_TEN) for t in range(N_TEN)]
+    opposite = [(t, (t + 4) % N_TEN) for t in range(N_TEN)]
     second = [(t, (t - turn(t)) % N_TEN) for t in range(N_TEN)]
 
     def send(x, perm):
@@ -218,20 +211,20 @@
     flat = jnp.broadcast_to(image.T[None], (N_SEC, IMG, BLK))
     mine = lax.all_to_all(flat, "section", 0, 0)
     wk, wv, text, upstream, mine = lax.optimization_barrier((wk, wv, text, upstream, mine))
-    got = send(mine, first)
+    img_opposite = send(mine, opposite)
+    img_first = send(mine, first)
+    img_second = send(mine, second)
     give = load(give_kernel, half, [dma((2, N_HALF))], me, wk, wv)
     peer = send(give, partner)
-    got, give = lax.optimization_barrier((got, give))
-    near = jnp.stack([mine, got])
-    wk, wv, text, upstream, near = lax.optimization_barrier((wk, wv, text, upstream, near))
-    far = send(near, second)
+    wk, wv, text, upstream, give = lax.optimization_barrier((wk, wv, text, upstream, give))
     own, text, upstream = load(
         load_kernel, (half, arr(BF16, *text.shape), arr(BF16, *upstream.shape)),
         [dma((2, N_HALF)), dma, dma], me, wk, wv, text, upstream,
     )
-    part = call(near_kernel, arr(F32, IMG, 4 * HD), 1 << 29, near, own, peer)
-    far, part = lax.optimization_barrier((far, part))
-    part, out_part = call(far_kernel, (arr(F32, IMG, 2 * HD),) * 2, 1 << 29, part, far, own, peer)
+    part, out_part = call(
+        project_kernel, (arr(F32, IMG, 2 * HD),) * 2, 1 << 30,
+        mine, img_first, img_second, img_opposite, own, peer,
+    )
     got_part = send(out_part, partner)
 
     probs, d_scores, rows, grads = call(
@@ -246,7 +239,6 @@
             functools.partial(term_kernel, slot), arr(dtype, N_SEC, BLK, IMG), 1 << 28, own, peer, grads, others
         )
 
-    opposite = [(t, (t + 4) % N_TEN) for t in range(N_TEN)]
     got_opposite = send(terms(3, BF16), opposite)
     got_first = send(terms(1, BF16), first)
     got_second = send(terms(2, BF16), second)

time: 105 us -> 103 us (0.981)
  the two profiles are of different devices: /device:TPU:6 before, /device:TPU:258 now
where the time goes in v1:
time: 103 us; the launch traced here: 102 us
  blocking collectives  50.7 us (49%)
  starting transfers between devices  26 us (25%)
  waiting for transfers between devices  11.2 us (11%)
  Pallas kernels  10.4 us (10%)
  between operations  2.08 us (2%)
    all_to_all x1, blocking collectives, shards(): mine = lax.all_to_all(flat, 'section', 0, 0)  29 us
    ppermute x9, starting transfers between devices, send(): return lax.ppermute(x, 'tensor', perm)  26 us
    all_to_all x1, blocking collectives, shards(): pieces = lax.all_to_all(total, 'section', 0, 0)  21.7 us
    ppermute x9, waiting for transfers between devices, send(): return lax.ppermute(x, 'tensor', perm)  11.2 us
    pallas_call x7, Pallas kernels, call(): pl.pallas_call(kernel, out_shape=outs, in_specs=[SMEM_SPEC if a.ndim == 1...  4.62 us
    pallas_call x2, Pallas kernels, load(): pl.pallas_call(kernel, out_shape=outs, in_specs=[SMEM_SPEC] + [pl.BlockSp...  3.51 us
    pallas_call x2, Pallas kernels, outside(): pl.pallas_call(kernel, out_shape=jax.ShapeDtypeStruct((TXT, GROUP * HD),...  2.26 us
  transfers between devices with their start and end apart: 9, of which 6 were waited for; matrix products, arithmetic and copies ran while one was open for 0% of the time, Pallas kernels for 5%

profile of v1, /device:TPU:258, one launch (start us, length us, event | category | flops | bytes accessed | tf_op | source)
XLA Modules:
  0.0 102.0 jit_solution(2152299873230764596)
XLA Ops:
  0.6 0.9 copy.10
  1.6 29.0 %all_to_all.10.a_ref = bf16[8,128,128]{2,1,0:T(8,128)(2,1)S(1)} all-to-all(bf16[8,128,128]{2,1,0:T(8,128)(2,1)S(1)} %broadcast_in_dim.12), channel_id=1, replica_groups=mesh['section'=8,'dp'=16,'tensor'=8] {'section'}, dimensions={0} | all-to-all | bytes 524288 | tf_op jit(solution)/shard_map/all_to_all | solution.py:212
  30.6 1.6 %shard_map.94 = bf16[2,4,8,128,128]{4,3,2,1,0:T(8,128)(2,1)S(1)} custom-call(s32[1]{0:T(128)} %bitcast.t_ref, bf16[8,8,128,128]{3,2,1,0:T(8,128)(2,1)} %bitcast.8, bf16[8,8,128,128]{3,2,1,0:T(8,128)(2,1)} %bitcast.10), custom_call_target="tpu_custom_call" | custom-call | bytes 6291456 | tf_op jit(solution)/shard_map/pallas_call | solution.py:178
  32.1 1.9 %collective-permute-start = (bf16[2,4,8,128,128]{4,3,2,1,0:T(8,128)(2,1)S(1)}, bf16[2,4,8,128,128]{4,3,2,1,0:T(8,128)(2,1)S(1)}, u32[]{:S(2)}, u32[]{:S(2)}) collective-permute-start(bf16[2,4,8,128,128]{4,3,2,1,0:T(8,128)(2,1)S(1)} %shard_map.94), channel_id=1, source_target_pairs={{0,1},{1,0},{2,3},{3,2},{4,5},{5,4},{6,7},{7,6},{8,9},{9,8},{10,11... | collective-permute-start | bytes 6291464 | tf_op jit(solution)/shard_map/ppermute | solution.py:205
  34.1 5.1 %collective-permute-start.3 = (bf16[8,128,128]{2,1,0:T(8,128)(2,1)S(1)}, bf16[8,128,128]{2,1,0:T(8,128)(2,1)S(1)}, u32[]{:S(2)}, u32[]{:S(2)}) collective-permute-start(bf16[8,128,128]{2,1,0:T(8,128)(2,1)S(1)} %all_to_all.10.a_ref), channel_id=1, source_target_pairs={{0,4},{1,5},{2,6},{3,7},{4,0},{5,1},{6,2},{7,3},{8,12},{9,13},{10,... | collective-permute-start | bytes 786440 | tf_op jit(solution)/shard_map/ppermute | solution.py:205
  39.2 3.0 %collective-permute-start.2 = (bf16[8,128,128]{2,1,0:T(8,128)(2,1)S(1)}, bf16[8,128,128]{2,1,0:T(8,128)(2,1)S(1)}, u32[]{:S(2)}, u32[]{:S(2)}) collective-permute-start(bf16[8,128,128]{2,1,0:T(8,128)(2,1)S(1)} %all_to_all.10.a_ref), channel_id=1, source_target_pairs={{0,6},{1,3},{2,4},{3,1},{4,2},{5,7},{6,0},{7,5},{8,14},{9,11},{10,... | collective-permute-start | bytes 786440 | tf_op jit(solution)/shard_map/ppermute | solution.py:205
  42.1 1.9 %collective-permute-start.1 = (bf16[8,128,128]{2,1,0:T(8,128)(2,1)S(1)}, bf16[8,128,128]{2,1,0:T(8,128)(2,1)S(1)}, u32[]{:S(2)}, u32[]{:S(2)}) collective-permute-start(bf16[8,128,128]{2,1,0:T(8,128)(2,1)S(1)} %all_to_all.10.a_ref), channel_id=1, source_target_pairs={{0,2},{1,7},{2,0},{3,5},{4,6},{5,3},{6,4},{7,1},{8,10},{9,15},{10,... | collective-permute-start | bytes 786440 | tf_op jit(solution)/shard_map/ppermute | solution.py:205
  44.1 1.9 %shard_map.95 = (bf16[2,4,8,128,128]{4,3,2,1,0:T(8,128)(2,1)S(1)}, bf16[256,1024]{1,0:T(8,128)(2,1)S(1)}, bf16[256,1024]{1,0:T(8,128)(2,1)S(1)}) custom-call(s32[1]{0:T(128)} %bitcast.t_ref, bf16[8,8,128,128]{3,2,1,0:T(8,128)(2,1)} %bitcast.9, bf16[8,8,128,128]{3,2,1,0:T(8,128)(2,1)} %bitcast.11, bf16[256,1024]{1,0:T(8,128)(2,1)} %bitcast.14, ...), custom_call_target="tpu_custom_call" | custom-call | bytes 6291456 | tf_op jit(solution)/shard_map/pallas_call | solution.py:178
  46.0 0.6 collective-permute-done.3.d_ref
  46.6 4.4 %collective-permute-done.2.c_ref = bf16[8,128,128]{2,1,0:T(8,128)(2,1)S(1)} collective-permute-done((bf16[8,128,128]{2,1,0:T(8,128)(2,1)S(1)}, bf16[8,128,128]{2,1,0:T(8,128)(2,1)S(1)}, u32[]{:S(2)}, u32[]{:S(2)}) %collective-permute-start.2) | collective-permute-done | bytes 262176 | tf_op jit(solution)/shard_map/ppermute | solution.py:205
  51.0 1.2 %collective-permute-done.1.b_ref = bf16[8,128,128]{2,1,0:T(8,128)(2,1)S(1)} collective-permute-done((bf16[8,128,128]{2,1,0:T(8,128)(2,1)S(1)}, bf16[8,128,128]{2,1,0:T(8,128)(2,1)S(1)}, u32[]{:S(2)}, u32[]{:S(2)}) %collective-permute-start.1) | collective-permute-done | bytes 262176 | tf_op jit(solution)/shard_map/ppermute | solution.py:205
  52.2 0.0 collective-permute-done.peer_ref
  52.2 0.7 shard_map.96
  52.9 1.9 %collective-permute-start.4 = (f32[128,256]{1,0:T(8,128)S(1)}, f32[128,256]{1,0:T(8,128)S(1)}, u32[]{:S(2)}, u32[]{:S(2)}) collective-permute-start(f32[128,256]{1,0:T(8,128)S(1)} %get-tuple-element.43), channel_id=1, source_target_pairs={{0,1},{1,0},{2,3},{3,2},{4,5},{5,4},{6,7},{7,6},{8,9},{9,8},{10,11... | collective-permute-start | bytes 393224 | tf_op jit(solution)/shard_map/ppermute | solution.py:205
  56.1 0.0 collective-permute-done.4.got_ref
  56.2 2.0 %shard_map.97 = (bf16[8,128,256]{2,1,0:T(8,128)(2,1)S(1)}, bf16[8,128,256]{2,1,0:T(8,128)(2,1)S(1)}, bf16[128,256]{1,0:T(8,128)(2,1)S(1)}, bf16[128,256]{1,0:T(8,128)(2,1)S(1)}) custom-call(s32[1]{0:T(128)S(6)} %copy.12.tiles_ref, f32[1]{0:T(128)S(6)} %copy.11.gate_ref, f32[128,256]{1,0:T(8,128)S(1)} %get-tuple-element.42.part_ref, ...), custom_call_target="tpu_custom_call" | custom-call | flops 1073741824 | bytes 1048576 | tf_op jit(solution)/shard_map/pallas_call | solution.py:131
  58.2 2.4 %collective-permute-start.5 = (bf16[128,256]{1,0:T(8,128)(2,1)S(1)}, bf16[128,256]{1,0:T(8,128)(2,1)S(1)}, u32[]{:S(2)}, u32[]{:S(2)}) collective-permute-start(bf16[128,256]{1,0:T(8,128)(2,1)S(1)} %get-tuple-element.46.grads_ref), channel_id=1, source_target_pairs={{0,1},{1,0},{2,3},{3,2},{4,5},{5,4},{6,7},{7,6},{8,9},{9,8},{10,11... | collective-permute-start | bytes 196616 | tf_op jit(solution)/shard_map/ppermute | solution.py:205
  60.6 0.9 collective-permute-done.5.others_ref
  61.5 0.4 shard_map.101
  61.9 4.6 %collective-permute-start.6 = (bf16[8,128,128]{2,1,0:T(8,128)(2,1)S(1)}, bf16[8,128,128]{2,1,0:T(8,128)(2,1)S(1)}, u32[]{:S(2)}, u32[]{:S(2)}) collective-permute-start(bf16[8,128,128]{2,1,0:T(8,128)(2,1)S(1)} %shard_map.101), channel_id=1, source_target_pairs={{0,4},{1,5},{2,6},{3,7},{4,0},{5,1},{6,2},{7,3},{8,12},{9,13},{10,... | collective-permute-start | bytes 786440 | tf_op jit(solution)/shard_map/ppermute | solution.py:205
  66.6 0.4 shard_map.102
  67.0 2.6 %collective-permute-start.7 = (bf16[8,128,128]{2,1,0:T(8,128)(2,1)S(1)}, bf16[8,128,128]{2,1,0:T(8,128)(2,1)S(1)}, u32[]{:S(2)}, u32[]{:S(2)}) collective-permute-start(bf16[8,128,128]{2,1,0:T(8,128)(2,1)S(1)} %shard_map.102), channel_id=1, source_target_pairs={{0,2},{1,7},{2,0},{3,5},{4,6},{5,3},{6,4},{7,1},{8,10},{9,15},{10,... | collective-permute-start | bytes 786440 | tf_op jit(solution)/shard_map/ppermute | solution.py:205
  69.6 0.4 shard_map.103
  70.0 2.6 %collective-permute-start.8 = (bf16[8,128,128]{2,1,0:T(8,128)(2,1)S(1)}, bf16[8,128,128]{2,1,0:T(8,128)(2,1)S(1)}, u32[]{:S(2)}, u32[]{:S(2)}) collective-permute-start(bf16[8,128,128]{2,1,0:T(8,128)(2,1)S(1)} %shard_map.103), channel_id=1, source_target_pairs={{0,6},{1,3},{2,4},{3,1},{4,2},{5,7},{6,0},{7,5},{8,14},{9,11},{10,... | collective-permute-start | bytes 786440 | tf_op jit(solution)/shard_map/ppermute | solution.py:205
  72.7 1.1 %shard_map.99 = bf16[256,1024]{1,0:T(8,128)(2,1)} custom-call(f32[1]{0:T(128)S(6)} %copy.11.gate_ref, bf16[8,128,256]{2,1,0:T(8,128)(2,1)S(1)} %get-tuple-element.47.probs_ref, bf16[128,256]{1,0:T(8,128)(2,1)S(1)} %get-tuple-element.48.rows_ref), custom_call_target="tpu_custom_call" | custom-call | flops 134217728 | bytes 1048576 | tf_op jit(solution)/shard_map/pallas_call | solution.py:142
  73.8 1.1 %shard_map.100 = bf16[256,1024]{1,0:T(8,128)(2,1)} custom-call(bf16[8,128,256]{2,1,0:T(8,128)(2,1)S(1)} %get-tuple-element.49.dscores_ref, bf16[128,256]{1,0:T(8,128)(2,1)S(1)} %get-tuple-element.48.rows_ref), custom_call_target="tpu_custom_call" | custom-call | flops 134217728 | bytes 1048576 | tf_op jit(solution)/shard_map/pallas_call | solution.py:142
  74.9 0.4 shard_map.98.keep_ref
  75.4 2.9 %collective-permute-done.7.b_ref = bf16[8,128,128]{2,1,0:T(8,128)(2,1)S(1)} collective-permute-done((bf16[8,128,128]{2,1,0:T(8,128)(2,1)S(1)}, bf16[8,128,128]{2,1,0:T(8,128)(2,1)S(1)}, u32[]{:S(2)}, u32[]{:S(2)}) %collective-permute-start.7) | collective-permute-done | bytes 262176 | tf_op jit(solution)/shard_map/ppermute | solution.py:205
  78.3 1.2 %collective-permute-done.8.c_ref = bf16[8,128,128]{2,1,0:T(8,128)(2,1)S(1)} collective-permute-done((bf16[8,128,128]{2,1,0:T(8,128)(2,1)S(1)}, bf16[8,128,128]{2,1,0:T(8,128)(2,1)S(1)}, u32[]{:S(2)}, u32[]{:S(2)}) %collective-permute-start.8) | collective-permute-done | bytes 262176 | tf_op jit(solution)/shard_map/ppermute | solution.py:205
  79.5 0.1 shard_map.104
  79.6 21.7 %all_to_all.11 = bf16[8,128,128]{2,1,0:T(8,128)(2,1)S(1)} all-to-all(bf16[8,128,128]{2,1,0:T(8,128)(2,1)S(1)} %shard_map.104), channel_id=1, replica_groups=mesh['section'=8,'dp'=16,'tensor'=8] {'section'}, dimensions={0} | all-to-all | bytes 524288 | tf_op jit(solution)/shard_map/all_to_all | solution.py:250
  101.3 0.7 reduce_sum.12
  (2 shorter events, 0.0 us)
Async XLA Ops:
  32.1 20.0 %collective-permute-start = (bf16[2,4,8,128,128]{4,3,2,1,0:T(8,128)(2,1)S(1)}, bf16[2,4,8,128,128]{4,3,2,1,0:T(8,128)(2,1)S(1)}, u32[]{:S(2)}, u32[]{:S(2)}) collective-permute-start(bf16[2,4,8,128,128]{4,3,2,1,0:T(8,128)(2,1)S(1)} %shard_map.94), channel_id=1, source_target_pairs={{0,1},{1,0},{2,3},{3,2},{4,5},{5,4},{6,7},{7,6},{8,9},{9,8},{10,11... | collective-permute-start | bytes 6291464 | tf_op jit(solution)/shard_map/ppermute | solution.py:205
  34.1 12.6 %collective-permute-start.3 = (bf16[8,128,128]{2,1,0:T(8,128)(2,1)S(1)}, bf16[8,128,128]{2,1,0:T(8,128)(2,1)S(1)}, u32[]{:S(2)}, u32[]{:S(2)}) collective-permute-start(bf16[8,128,128]{2,1,0:T(8,128)(2,1)S(1)} %all_to_all.10.a_ref), channel_id=1, source_target_pairs={{0,4},{1,5},{2,6},{3,7},{4,0},{5,1},{6,2},{7,3},{8,12},{9,13},{10,... | collective-permute-start | bytes 786440 | tf_op jit(solution)/shard_map/ppermute | solution.py:205
  39.2 11.8 %collective-permute-start.2 = (bf16[8,128,128]{2,1,0:T(8,128)(2,1)S(1)}, bf16[8,128,128]{2,1,0:T(8,128)(2,1)S(1)}, u32[]{:S(2)}, u32[]{:S(2)}) collective-permute-start(bf16[8,128,128]{2,1,0:T(8,128)(2,1)S(1)} %all_to_all.10.a_ref), channel_id=1, source_target_pairs={{0,6},{1,3},{2,4},{3,1},{4,2},{5,7},{6,0},{7,5},{8,14},{9,11},{10,... | collective-permute-start | bytes 786440 | tf_op jit(solution)/shard_map/ppermute | solution.py:205
  42.1 10.0 %collective-permute-start.1 = (bf16[8,128,128]{2,1,0:T(8,128)(2,1)S(1)}, bf16[8,128,128]{2,1,0:T(8,128)(2,1)S(1)}, u32[]{:S(2)}, u32[]{:S(2)}) collective-permute-start(bf16[8,128,128]{2,1,0:T(8,128)(2,1)S(1)} %all_to_all.10.a_ref), channel_id=1, source_target_pairs={{0,2},{1,7},{2,0},{3,5},{4,6},{5,3},{6,4},{7,1},{8,10},{9,15},{10,... | collective-permute-start | bytes 786440 | tf_op jit(solution)/shard_map/ppermute | solution.py:205
  52.9 3.2 %collective-permute-start.4 = (f32[128,256]{1,0:T(8,128)S(1)}, f32[128,256]{1,0:T(8,128)S(1)}, u32[]{:S(2)}, u32[]{:S(2)}) collective-permute-start(f32[128,256]{1,0:T(8,128)S(1)} %get-tuple-element.43), channel_id=1, source_target_pairs={{0,1},{1,0},{2,3},{3,2},{4,5},{5,4},{6,7},{7,6},{8,9},{9,8},{10,11... | collective-permute-start | bytes 393224 | tf_op jit(solution)/shard_map/ppermute | solution.py:205
  58.2 3.3 %collective-permute-start.5 = (bf16[128,256]{1,0:T(8,128)(2,1)S(1)}, bf16[128,256]{1,0:T(8,128)(2,1)S(1)}, u32[]{:S(2)}, u32[]{:S(2)}) collective-permute-start(bf16[128,256]{1,0:T(8,128)(2,1)S(1)} %get-tuple-element.46.grads_ref), channel_id=1, source_target_pairs={{0,1},{1,0},{2,3},{3,2},{4,5},{5,4},{6,7},{7,6},{8,9},{9,8},{10,11... | collective-permute-start | bytes 196616 | tf_op jit(solution)/shard_map/ppermute | solution.py:205
  61.9 13.4 %collective-permute-start.6 = (bf16[8,128,128]{2,1,0:T(8,128)(2,1)S(1)}, bf16[8,128,128]{2,1,0:T(8,128)(2,1)S(1)}, u32[]{:S(2)}, u32[]{:S(2)}) collective-permute-start(bf16[8,128,128]{2,1,0:T(8,128)(2,1)S(1)} %shard_map.101), channel_id=1, source_target_pairs={{0,4},{1,5},{2,6},{3,7},{4,0},{5,1},{6,2},{7,3},{8,12},{9,13},{10,... | collective-permute-start | bytes 786440 | tf_op jit(solution)/shard_map/ppermute | solution.py:205
  67.0 11.3 %collective-permute-start.7 = (bf16[8,128,128]{2,1,0:T(8,128)(2,1)S(1)}, bf16[8,128,128]{2,1,0:T(8,128)(2,1)S(1)}, u32[]{:S(2)}, u32[]{:S(2)}) collective-permute-start(bf16[8,128,128]{2,1,0:T(8,128)(2,1)S(1)} %shard_map.102), channel_id=1, source_target_pairs={{0,2},{1,7},{2,0},{3,5},{4,6},{5,3},{6,4},{7,1},{8,10},{9,15},{10,... | collective-permute-start | bytes 786440 | tf_op jit(solution)/shard_map/ppermute | solution.py:205
  70.0 9.5 %collective-permute-start.8 = (bf16[8,128,128]{2,1,0:T(8,128)(2,1)S(1)}, bf16[8,128,128]{2,1,0:T(8,128)(2,1)S(1)}, u32[]{:S(2)}, u32[]{:S(2)}) collective-permute-start(bf16[8,128,128]{2,1,0:T(8,128)(2,1)S(1)} %shard_map.103), channel_id=1, source_target_pairs={{0,6},{1,3},{2,4},{3,1},{4,2},{5,7},{6,0},{7,5},{8,14},{9,11},{10,... | collective-permute-start | bytes 786440 | tf_op jit(solution)/shard_map/ppermute | solution.py:205

commit v2 on v1

--- a/solution.py
+++ b/solution.py
@@ -45,7 +45,11 @@
         for j in range(0, N_SEC, 2):
             left = jnp.concatenate([img_ref[j], img_ref[j + 1]], axis=1)
             right = jnp.concatenate(
-                [ref[kv, slot, j : j + 2].reshape(2 * BLK, HD) for ref in (own_ref, peer_ref) for kv in range(2)],
+                [
+                    jnp.concatenate([ref[kv, slot, j // 2], ref[kv, slot, j // 2 + N_SEC // 2]], axis=0)
+                    for ref in (own_ref, peer_ref)
+                    for kv in range(2)
+                ],
                 axis=1,
             )
             part = dot(left, right, NN)
@@ -102,7 +106,30 @@
 
 def join_kernel(keep_ref, a_ref, b_ref, c_ref, out_ref):
     total = keep_ref[...] + a_ref[...].astype(F32)
-    out_ref[...] = (total + b_ref[...].astype(F32) + c_ref[...].astype(F32)).astype(BF16)
+    total = (total + b_ref[...].astype(F32) + c_ref[...].astype(F32)).astype(BF16)
+    for j in range(N_SEC // 2):
+        out_ref[j, 0] = total[j]
+        out_ref[j, 1] = total[j + N_SEC // 2]
+
+
+def pair_kernel(layer_ref, own_ref, passed_ref, out_ref):
+    upper = jnp.full((BLK, IMG), layer_ref[0], jnp.int32) >= N_SEC // 2
+    own = own_ref[...].astype(F32)
+    passed = passed_ref[...].astype(F32)
+    low = jnp.where(upper, passed, own).T.astype(BF16)
+    high = jnp.where(upper, own, passed).T.astype(BF16)
+    for n in range(N_SEC // 2):
+        out_ref[n, 0] = low
+        out_ref[n, 1] = high
+
+
+def half_kernel(layer_ref, in_ref, keep_ref, send_ref):
+    total = in_ref[0].astype(F32)
+    for n in range(1, N_SEC // 2):
+        total = total + in_ref[n].astype(F32)
+    upper = jnp.full((BLK, IMG), layer_ref[0], jnp.int32) >= N_SEC // 2
+    keep_ref[...] = jnp.where(upper, total[1], total[0])
+    send_ref[...] = jnp.where(upper, total[0], total[1]).astype(BF16)
 
 
 def attended_kernel(gate_ref, probs_ref, rows_ref, out_ref):
@@ -196,6 +223,9 @@
     def turn(t):
         return 2 - 4 * (((t >> 1) + t) & 1)
 
+    across = [(s, s ^ 4) for s in range(N_SEC)]
+    groups = [[0, 1, 2, 3], [4, 5, 6, 7]]
+    layer = lax.axis_index("section").astype(jnp.int32).reshape(1)
     partner = [(t, t ^ 1) for t in range(N_TEN)]
     first = [(t, (t + turn(t)) % N_TEN) for t in range(N_TEN)]
     opposite = [(t, (t + 4) % N_TEN) for t in range(N_TEN)]
@@ -207,16 +237,24 @@
     dma = pltpu.SemaphoreType.DMA
     half = arr(BF16, 2, N_HALF, N_SEC, BLK, HD)
 
-    image, me, gates, tiles = lax.optimization_barrier((image, me, gates, tiles))
-    flat = jnp.broadcast_to(image.T[None], (N_SEC, IMG, BLK))
-    mine = lax.all_to_all(flat, "section", 0, 0)
-    wk, wv, text, upstream, mine = lax.optimization_barrier((wk, wv, text, upstream, mine))
+    image, me, gates, tiles, layer = lax.optimization_barrier((image, me, gates, tiles, layer))
+    passed = lax.ppermute(image, "section", across)
+    give = load(give_kernel, half, [dma((2, N_HALF))], me, wk, wv)
+    peer = send(give, partner)
+    passed, give = lax.optimization_barrier((passed, give))
+    flat = pl.pallas_call(
+        pair_kernel,
+        name="pair",
+        out_shape=arr(BF16, N_SEC // 2, 2, IMG, BLK),
+        in_specs=[SMEM_SPEC, VMEM_SPEC, VMEM_SPEC],
+        out_specs=VMEM_SPEC,
+        compiler_params=pltpu.CompilerParams(vmem_limit_bytes=VMEM_GRANT),
+    )(layer, image, pltpu.with_memory_space_constraint(passed, pltpu.VMEM))
+    mine = lax.all_to_all(flat, "section", 0, 0, axis_index_groups=groups).reshape(N_SEC, IMG, BLK)
     img_opposite = send(mine, opposite)
     img_first = send(mine, first)
     img_second = send(mine, second)
-    give = load(give_kernel, half, [dma((2, N_HALF))], me, wk, wv)
-    peer = send(give, partner)
-    wk, wv, text, upstream, give = lax.optimization_barrier((wk, wv, text, upstream, give))
+    wk, wv, text, upstream, mine = lax.optimization_barrier((wk, wv, text, upstream, mine))
     own, text, upstream = load(
         load_kernel, (half, arr(BF16, *text.shape), arr(BF16, *upstream.shape)),
         [dma((2, N_HALF)), dma, dma], me, wk, wv, text, upstream,
@@ -246,9 +284,13 @@
     attended = outside(attended_kernel, gates, probs, rows)
     d_query = outside(dquery_kernel, d_scores, rows)
     keep, attended, d_query = lax.optimization_barrier((keep, attended, d_query))
-    total = call(join_kernel, arr(BF16, N_SEC, BLK, IMG), 1 << 20, keep, got_opposite, got_first, got_second)
-    pieces = lax.all_to_all(total, "section", 0, 0)
-    grad = jnp.sum(pieces.astype(F32), axis=0).astype(BF16)
+    total = call(join_kernel, arr(BF16, N_SEC // 2, 2, BLK, IMG), 1 << 20, keep, got_opposite, got_first, got_second)
+    pieces = lax.all_to_all(total, "section", 0, 0, axis_index_groups=groups)
+    stay, leave = call(
+        half_kernel, (arr(F32, BLK, IMG), arr(BF16, BLK, IMG)), 1 << 20,
+        layer, pieces,
+    )
+    grad = (stay + lax.ppermute(leave, "section", across).astype(F32)).astype(BF16)
     return (attended[None], d_query[None], grad)
 
 

time: 103 us -> 102 us (level)
  the two profiles are of different devices: /device:TPU:258 before, /device:TPU:24 now
where the time goes in v2:
time: 102 us
  starting transfers between devices  42.5 us (42%)
  blocking collectives  27.3 us (27%)
  waiting for transfers between devices  18.5 us (18%)
  Pallas kernels  10.5 us (10%)
  between operations  2.12 us (2%)
    ppermute x9, starting transfers between devices, send(): return lax.ppermute(x, 'tensor', perm)  30.6 us
    all_to_all x1, blocking collectives, shards(): lax.all_to_all(flat, 'section', 0, 0, axis_index_groups=groups)  14.8 us
    all_to_all x1, blocking collectives, shards(): pieces = lax.all_to_all(total, 'section', 0, 0, axis_index_groups=groups)  12.6 us
    ppermute x9, waiting for transfers between devices, send(): return lax.ppermute(x, 'tensor', perm)  9.29 us
    ppermute x1, starting transfers between devices, shards(): passed = lax.ppermute(image, 'section', across)  9.1 us
    ppermute x1, waiting for transfers between devices, shards(): lax.ppermute(leave, 'section', across).astype(F32)  7.2 us
    pallas_call x8, Pallas kernels, call(): pl.pallas_call(kernel, out_shape=outs, in_specs=[SMEM_SPEC if a.ndim == 1...  4.66 us
    pallas_call x2, Pallas kernels, load(): pl.pallas_call(kernel, out_shape=outs, in_specs=[SMEM_SPEC] + [pl.BlockSp...  3.52 us
  transfers between devices with their start and end apart: 11, of which 7 were waited for; matrix products, arithmetic and copies ran while one was open for 0% of the time, Pallas kernels for 5%

profile of v2, /device:TPU:24, one launch (start us, length us, event | category | flops | bytes accessed | tf_op | source)
XLA Modules:
  0.0 101.7 jit_solution(13244035525559322676)
XLA Ops:
  0.6 1.6 %shard_map.94 = bf16[2,4,8,128,128]{4,3,2,1,0:T(8,128)(2,1)S(1)} custom-call(s32[1]{0:T(128)} %bitcast.t_ref, bf16[8,8,128,128]{3,2,1,0:T(8,128)(2,1)} %bitcast.13, bf16[8,8,128,128]{3,2,1,0:T(8,128)(2,1)} %bitcast.15), custom_call_target="tpu_custom_call" | custom-call | bytes 6291456 | tf_op jit(solution)/shard_map/pallas_call | solution.py:205
  2.2 1.9 %collective-permute-start.1 = (bf16[2,4,8,128,128]{4,3,2,1,0:T(8,128)(2,1)S(1)}, bf16[2,4,8,128,128]{4,3,2,1,0:T(8,128)(2,1)S(1)}, u32[]{:S(2)}, u32[]{:S(2)}) collective-permute-start(bf16[2,4,8,128,128]{4,3,2,1,0:T(8,128)(2,1)S(1)} %shard_map.94), channel_id=1, source_target_pairs={{0,1},{1,0},{2,3},{3,2},{4,5},{5,4},{6,7},{7,6},{8,9},{9,8},{10,11... | collective-permute-start | bytes 6291464 | tf_op jit(solution)/shard_map/ppermute | solution.py:235
  4.2 9.1 %collective-permute-start = (bf16[128,128]{1,0:T(8,128)(2,1)S(1)}, bf16[128,128]{1,0:T(8,128)(2,1)S(1)}, u32[]{:S(2)}, u32[]{:S(2)}) collective-permute-start(bf16[128,128]{1,0:T(8,128)(2,1)S(1)} %copy-done), channel_id=1, source_target_pairs={{0,512},{128,640},{256,768},{384,896},{512,0},{640,128},{768,256},... | collective-permute-start | bytes 98312 | tf_op jit(solution)/shard_map/ppermute | solution.py:241
  13.3 2.0 %collective-permute-done.passed_ref = bf16[128,128]{1,0:T(8,128)(2,1)S(1)} collective-permute-done((bf16[128,128]{1,0:T(8,128)(2,1)S(1)}, bf16[128,128]{1,0:T(8,128)(2,1)S(1)}, u32[]{:S(2)}, u32[]{:S(2)}) %collective-permute-start) | collective-permute-done | bytes 32800 | tf_op jit(solution)/shard_map/ppermute | solution.py:241
  15.4 14.8 %all_to_all.10 = bf16[4,2,128,128]{3,2,1,0:T(8,128)(2,1)S(1)} all-to-all(bf16[4,2,128,128]{3,2,1,0:T(8,128)(2,1)S(1)} %pair.1), channel_id=1, replica_groups={{0,128,256,384},{512,640,768,896},{1,129,257,385},{513,641,769,897},{2,..., dimensions={0} | all-to-all | bytes 524288 | tf_op jit(solution)/shard_map/all_to_all | solution.py:253
  30.2 3.1 %collective-permute-start.4 = (bf16[8,128,128]{2,1,0:T(8,128)(2,1)S(1)}, bf16[8,128,128]{2,1,0:T(8,128)(2,1)S(1)}, u32[]{:S(2)}, u32[]{:S(2)}) collective-permute-start(bf16[8,128,128]{2,1,0:T(8,128)(2,1)S(1)} %bitcast.9), channel_id=1, source_target_pairs={{0,4},{1,5},{2,6},{3,7},{4,0},{5,1},{6,2},{7,3},{8,12},{9,13},{10,... | collective-permute-start | bytes 786440 | tf_op jit(solution)/shard_map/ppermute | solution.py:235
  33.3 8.4 %collective-permute-start.3 = (bf16[8,128,128]{2,1,0:T(8,128)(2,1)S(1)}, bf16[8,128,128]{2,1,0:T(8,128)(2,1)S(1)}, u32[]{:S(2)}, u32[]{:S(2)}) collective-permute-start(bf16[8,128,128]{2,1,0:T(8,128)(2,1)S(1)} %bitcast.10), channel_id=1, source_target_pairs={{0,6},{1,3},{2,4},{3,1},{4,2},{5,7},{6,0},{7,5},{8,14},{9,11},{10,... | collective-permute-start | bytes 786440 | tf_op jit(solution)/shard_map/ppermute | solution.py:235
  41.7 2.8 %collective-permute-start.2 = (bf16[8,128,128]{2,1,0:T(8,128)(2,1)S(1)}, bf16[8,128,128]{2,1,0:T(8,128)(2,1)S(1)}, u32[]{:S(2)}, u32[]{:S(2)}) collective-permute-start(bf16[8,128,128]{2,1,0:T(8,128)(2,1)S(1)} %bitcast.11), channel_id=1, source_target_pairs={{0,2},{1,7},{2,0},{3,5},{4,6},{5,3},{6,4},{7,1},{8,10},{9,15},{10,... | collective-permute-start | bytes 786440 | tf_op jit(solution)/shard_map/ppermute | solution.py:235
  44.5 1.9 %shard_map.95 = (bf16[2,4,8,128,128]{4,3,2,1,0:T(8,128)(2,1)S(1)}, bf16[256,1024]{1,0:T(8,128)(2,1)S(1)}, bf16[256,1024]{1,0:T(8,128)(2,1)S(1)}) custom-call(s32[1]{0:T(128)} %bitcast.t_ref, bf16[8,8,128,128]{3,2,1,0:T(8,128)(2,1)} %bitcast.14, bf16[8,8,128,128]{3,2,1,0:T(8,128)(2,1)} %bitcast.16, bf16[256,1024]{1,0:T(8,128)(2,1)} %bitcast.19, ...), custom_call_target="tpu_custom_call" | custom-call | bytes 6291456 | tf_op jit(solution)/shard_map/pallas_call | solution.py:205
  46.5 3.3 %collective-permute-done.3.c_ref = bf16[8,128,128]{2,1,0:T(8,128)(2,1)S(1)} collective-permute-done((bf16[8,128,128]{2,1,0:T(8,128)(2,1)S(1)}, bf16[8,128,128]{2,1,0:T(8,128)(2,1)S(1)}, u32[]{:S(2)}, u32[]{:S(2)}) %collective-permute-start.3) | collective-permute-done | bytes 262176 | tf_op jit(solution)/shard_map/ppermute | solution.py:235
  49.8 0.2 collective-permute-done.2.b_ref
  50.0 0.7 shard_map.96
  50.8 1.9 %collective-permute-start.5 = (f32[128,256]{1,0:T(8,128)S(1)}, f32[128,256]{1,0:T(8,128)S(1)}, u32[]{:S(2)}, u32[]{:S(2)}) collective-permute-start(f32[128,256]{1,0:T(8,128)S(1)} %get-tuple-element.41), channel_id=1, source_target_pairs={{0,1},{1,0},{2,3},{3,2},{4,5},{5,4},{6,7},{7,6},{8,9},{9,8},{10,11... | collective-permute-start | bytes 393224 | tf_op jit(solution)/shard_map/ppermute | solution.py:235
  54.0 2.0 %shard_map.97 = (bf16[8,128,256]{2,1,0:T(8,128)(2,1)S(1)}, bf16[8,128,256]{2,1,0:T(8,128)(2,1)S(1)}, bf16[128,256]{1,0:T(8,128)(2,1)S(1)}, bf16[128,256]{1,0:T(8,128)(2,1)S(1)}) custom-call(s32[1]{0:T(128)S(6)} %copy.11.tiles_ref, f32[1]{0:T(128)S(6)} %copy.10.gate_ref, f32[128,256]{1,0:T(8,128)S(1)} %get-tuple-element.40.part_ref, ...), custom_call_target="tpu_custom_call" | custom-call | flops 1073741824 | bytes 1048576 | tf_op jit(solution)/shard_map/pallas_call | solution.py:158
  56.0 2.4 %collective-permute-start.6 = (bf16[128,256]{1,0:T(8,128)(2,1)S(1)}, bf16[128,256]{1,0:T(8,128)(2,1)S(1)}, u32[]{:S(2)}, u32[]{:S(2)}) collective-permute-start(bf16[128,256]{1,0:T(8,128)(2,1)S(1)} %get-tuple-element.44.grads_ref), channel_id=1, source_target_pairs={{0,1},{1,0},{2,3},{3,2},{4,5},{5,4},{6,7},{7,6},{8,9},{9,8},{10,11... | collective-permute-start | bytes 196616 | tf_op jit(solution)/shard_map/ppermute | solution.py:235
  58.4 0.9 collective-permute-done.6.others_ref
  59.3 0.4 shard_map.101
  59.8 4.8 %collective-permute-start.7 = (bf16[8,128,128]{2,1,0:T(8,128)(2,1)S(1)}, bf16[8,128,128]{2,1,0:T(8,128)(2,1)S(1)}, u32[]{:S(2)}, u32[]{:S(2)}) collective-permute-start(bf16[8,128,128]{2,1,0:T(8,128)(2,1)S(1)} %shard_map.101), channel_id=1, source_target_pairs={{0,4},{1,5},{2,6},{3,7},{4,0},{5,1},{6,2},{7,3},{8,12},{9,13},{10,... | collective-permute-start | bytes 786440 | tf_op jit(solution)/shard_map/ppermute | solution.py:235
  64.6 0.4 shard_map.102
  65.0 3.3 %collective-permute-start.8 = (bf16[8,128,128]{2,1,0:T(8,128)(2,1)S(1)}, bf16[8,128,128]{2,1,0:T(8,128)(2,1)S(1)}, u32[]{:S(2)}, u32[]{:S(2)}) collective-permute-start(bf16[8,128,128]{2,1,0:T(8,128)(2,1)S(1)} %shard_map.102), channel_id=1, source_target_pairs={{0,2},{1,7},{2,0},{3,5},{4,6},{5,3},{6,4},{7,1},{8,10},{9,15},{10,... | collective-permute-start | bytes 786440 | tf_op jit(solution)/shard_map/ppermute | solution.py:235
  68.3 0.4 shard_map.103
  68.8 1.9 %collective-permute-start.9 = (bf16[8,128,128]{2,1,0:T(8,128)(2,1)S(1)}, bf16[8,128,128]{2,1,0:T(8,128)(2,1)S(1)}, u32[]{:S(2)}, u32[]{:S(2)}) collective-permute-start(bf16[8,128,128]{2,1,0:T(8,128)(2,1)S(1)} %shard_map.103), channel_id=1, source_target_pairs={{0,6},{1,3},{2,4},{3,1},{4,2},{5,7},{6,0},{7,5},{8,14},{9,11},{10,... | collective-permute-start | bytes 786440 | tf_op jit(solution)/shard_map/ppermute | solution.py:235
  70.7 1.1 %shard_map.99 = bf16[256,1024]{1,0:T(8,128)(2,1)} custom-call(f32[1]{0:T(128)S(6)} %copy.10.gate_ref, bf16[8,128,256]{2,1,0:T(8,128)(2,1)S(1)} %get-tuple-element.45.probs_ref, bf16[128,256]{1,0:T(8,128)(2,1)S(1)} %get-tuple-element.46.rows_ref), custom_call_target="tpu_custom_call" | custom-call | flops 134217728 | bytes 1048576 | tf_op jit(solution)/shard_map/pallas_call | solution.py:169
  71.8 1.1 %shard_map.100 = bf16[256,1024]{1,0:T(8,128)(2,1)} custom-call(bf16[8,128,256]{2,1,0:T(8,128)(2,1)S(1)} %get-tuple-element.47.dscores_ref, bf16[128,256]{1,0:T(8,128)(2,1)S(1)} %get-tuple-element.46.rows_ref), custom_call_target="tpu_custom_call" | custom-call | flops 134217728 | bytes 1048576 | tf_op jit(solution)/shard_map/pallas_call | solution.py:169
  73.0 0.4 shard_map.98.keep_ref
  73.4 4.4 %collective-permute-done.8.b_ref = bf16[8,128,128]{2,1,0:T(8,128)(2,1)S(1)} collective-permute-done((bf16[8,128,128]{2,1,0:T(8,128)(2,1)S(1)}, bf16[8,128,128]{2,1,0:T(8,128)(2,1)S(1)}, u32[]{:S(2)}, u32[]{:S(2)}) %collective-permute-start.8) | collective-permute-done | bytes 262176 | tf_op jit(solution)/shard_map/ppermute | solution.py:235
  77.8 0.5 collective-permute-done.9.c_ref
  78.3 0.1 shard_map.104
  78.4 12.6 %all_to_all.11.in_ref = bf16[4,2,128,128]{3,2,1,0:T(8,128)(2,1)S(1)} all-to-all(bf16[4,2,128,128]{3,2,1,0:T(8,128)(2,1)S(1)} %shard_map.104), channel_id=1, replica_groups={{0,128,256,384},{512,640,768,896},{1,129,257,385},{513,641,769,897},{2,..., dimensions={0} | all-to-all | bytes 524288 | tf_op jit(solution)/shard_map/all_to_all | solution.py:288
  91.0 2.9 %collective-permute-start.10 = (bf16[128,128]{1,0:T(8,128)(2,1)S(1)}, bf16[128,128]{1,0:T(8,128)(2,1)S(1)}, u32[]{:S(2)}, u32[]{:S(2)}) collective-permute-start(bf16[128,128]{1,0:T(8,128)(2,1)S(1)} %get-tuple-element.52), channel_id=1, source_target_pairs={{0,512},{128,640},{256,768},{384,896},{512,0},{640,128},{768,256},... | collective-permute-start | bytes 98312 | tf_op jit(solution)/shard_map/ppermute | solution.py:293
  93.8 7.2 %collective-permute-done.10 = bf16[128,128]{1,0:T(8,128)(2,1)S(1)} collective-permute-done((bf16[128,128]{1,0:T(8,128)(2,1)S(1)}, bf16[128,128]{1,0:T(8,128)(2,1)S(1)}, u32[]{:S(2)}, u32[]{:S(2)}) %collective-permute-start.10) | collective-permute-done | bytes 32800 | tf_op jit(solution)/shard_map/ppermute | solution.py:293
  101.0 0.6 add_convert_fusion
  (8 shorter events, 0.2 us)
Async XLA Ops:
  0.6 3.5 %copy-start = (bf16[128,128]{1,0:T(8,128)(2,1)S(1)}, bf16[128,128]{1,0:T(8,128)(2,1)}, u32[]{:S(2)}) copy-start(bf16[128,128]{1,0:T(8,128)(2,1)} %own_ref) | copy-start | bytes 98308
  2.2 47.8 %collective-permute-start.1 = (bf16[2,4,8,128,128]{4,3,2,1,0:T(8,128)(2,1)S(1)}, bf16[2,4,8,128,128]{4,3,2,1,0:T(8,128)(2,1)S(1)}, u32[]{:S(2)}, u32[]{:S(2)}) collective-permute-start(bf16[2,4,8,128,128]{4,3,2,1,0:T(8,128)(2,1)S(1)} %shard_map.94), channel_id=1, source_target_pairs={{0,1},{1,0},{2,3},{3,2},{4,5},{5,4},{6,7},{7,6},{8,9},{9,8},{10,11... | collective-permute-start | bytes 6291464 | tf_op jit(solution)/shard_map/ppermute | solution.py:235
  4.2 11.1 %collective-permute-start = (bf16[128,128]{1,0:T(8,128)(2,1)S(1)}, bf16[128,128]{1,0:T(8,128)(2,1)S(1)}, u32[]{:S(2)}, u32[]{:S(2)}) collective-permute-start(bf16[128,128]{1,0:T(8,128)(2,1)S(1)} %copy-done), channel_id=1, source_target_pairs={{0,512},{128,640},{256,768},{384,896},{512,0},{640,128},{768,256},... | collective-permute-start | bytes 98312 | tf_op jit(solution)/shard_map/ppermute | solution.py:241
  30.2 16.3 %collective-permute-start.4 = (bf16[8,128,128]{2,1,0:T(8,128)(2,1)S(1)}, bf16[8,128,128]{2,1,0:T(8,128)(2,1)S(1)}, u32[]{:S(2)}, u32[]{:S(2)}) collective-permute-start(bf16[8,128,128]{2,1,0:T(8,128)(2,1)S(1)} %bitcast.9), channel_id=1, source_target_pairs={{0,4},{1,5},{2,6},{3,7},{4,0},{5,1},{6,2},{7,3},{8,12},{9,13},{10,... | collective-permute-start | bytes 786440 | tf_op jit(solution)/shard_map/ppermute | solution.py:235
  33.3 16.4 %collective-permute-start.3 = (bf16[8,128,128]{2,1,0:T(8,128)(2,1)S(1)}, bf16[8,128,128]{2,1,0:T(8,128)(2,1)S(1)}, u32[]{:S(2)}, u32[]{:S(2)}) collective-permute-start(bf16[8,128,128]{2,1,0:T(8,128)(2,1)S(1)} %bitcast.10), channel_id=1, source_target_pairs={{0,6},{1,3},{2,4},{3,1},{4,2},{5,7},{6,0},{7,5},{8,14},{9,11},{10,... | collective-permute-start | bytes 786440 | tf_op jit(solution)/shard_map/ppermute | solution.py:235
  41.7 8.3 %collective-permute-start.2 = (bf16[8,128,128]{2,1,0:T(8,128)(2,1)S(1)}, bf16[8,128,128]{2,1,0:T(8,128)(2,1)S(1)}, u32[]{:S(2)}, u32[]{:S(2)}) collective-permute-start(bf16[8,128,128]{2,1,0:T(8,128)(2,1)S(1)} %bitcast.11), channel_id=1, source_target_pairs={{0,2},{1,7},{2,0},{3,5},{4,6},{5,3},{6,4},{7,1},{8,10},{9,15},{10,... | collective-permute-start | bytes 786440 | tf_op jit(solution)/shard_map/ppermute | solution.py:235
  50.8 3.2 %collective-permute-start.5 = (f32[128,256]{1,0:T(8,128)S(1)}, f32[128,256]{1,0:T(8,128)S(1)}, u32[]{:S(2)}, u32[]{:S(2)}) collective-permute-start(f32[128,256]{1,0:T(8,128)S(1)} %get-tuple-element.41), channel_id=1, source_target_pairs={{0,1},{1,0},{2,3},{3,2},{4,5},{5,4},{6,7},{7,6},{8,9},{9,8},{10,11... | collective-permute-start | bytes 393224 | tf_op jit(solution)/shard_map/ppermute | solution.py:235
  56.0 3.3 %collective-permute-start.6 = (bf16[128,256]{1,0:T(8,128)(2,1)S(1)}, bf16[128,256]{1,0:T(8,128)(2,1)S(1)}, u32[]{:S(2)}, u32[]{:S(2)}) collective-permute-start(bf16[128,256]{1,0:T(8,128)(2,1)S(1)} %get-tuple-element.44.grads_ref), channel_id=1, source_target_pairs={{0,1},{1,0},{2,3},{3,2},{4,5},{5,4},{6,7},{7,6},{8,9},{9,8},{10,11... | collective-permute-start | bytes 196616 | tf_op jit(solution)/shard_map/ppermute | solution.py:235
  59.8 13.6 %collective-permute-start.7 = (bf16[8,128,128]{2,1,0:T(8,128)(2,1)S(1)}, bf16[8,128,128]{2,1,0:T(8,128)(2,1)S(1)}, u32[]{:S(2)}, u32[]{:S(2)}) collective-permute-start(bf16[8,128,128]{2,1,0:T(8,128)(2,1)S(1)} %shard_map.101), channel_id=1, source_target_pairs={{0,4},{1,5},{2,6},{3,7},{4,0},{5,1},{6,2},{7,3},{8,12},{9,13},{10,... | collective-permute-start | bytes 786440 | tf_op jit(solution)/shard_map/ppermute | solution.py:235
  65.0 12.7 %collective-permute-start.8 = (bf16[8,128,128]{2,1,0:T(8,128)(2,1)S(1)}, bf16[8,128,128]{2,1,0:T(8,128)(2,1)S(1)}, u32[]{:S(2)}, u32[]{:S(2)}) collective-permute-start(bf16[8,128,128]{2,1,0:T(8,128)(2,1)S(1)} %shard_map.102), channel_id=1, source_target_pairs={{0,2},{1,7},{2,0},{3,5},{4,6},{5,3},{6,4},{7,1},{8,10},{9,15},{10,... | collective-permute-start | bytes 786440 | tf_op jit(solution)/shard_map/ppermute | solution.py:235
  68.8 9.5 %collective-permute-start.9 = (bf16[8,128,128]{2,1,0:T(8,128)(2,1)S(1)}, bf16[8,128,128]{2,1,0:T(8,128)(2,1)S(1)}, u32[]{:S(2)}, u32[]{:S(2)}) collective-permute-start(bf16[8,128,128]{2,1,0:T(8,128)(2,1)S(1)} %shard_map.103), channel_id=1, source_target_pairs={{0,6},{1,3},{2,4},{3,1},{4,2},{5,7},{6,0},{7,5},{8,14},{9,11},{10,... | collective-permute-start | bytes 786440 | tf_op jit(solution)/shard_map/ppermute | solution.py:235
  91.0 10.1 %collective-permute-start.10 = (bf16[128,128]{1,0:T(8,128)(2,1)S(1)}, bf16[128,128]{1,0:T(8,128)(2,1)S(1)}, u32[]{:S(2)}, u32[]{:S(2)}) collective-permute-start(bf16[128,128]{1,0:T(8,128)(2,1)S(1)} %get-tuple-element.52), channel_id=1, source_target_pairs={{0,512},{128,640},{256,768},{384,896},{512,0},{640,128},{768,256},... | collective-permute-start | bytes 98312 | tf_op jit(solution)/shard_map/ppermute | solution.py:293

commit v3 on v2

--- a/solution.py
+++ b/solution.py
@@ -39,9 +39,8 @@
     return [t, (t + step) % N_TEN, (t - step) % N_TEN, (t + 4) % N_TEN]
 
 
-def project_kernel(a_ref, b_ref, c_ref, d_ref, own_ref, peer_ref, out_ref, send_ref):
-    total = None
-    for slot, img_ref in enumerate((a_ref, b_ref, c_ref, d_ref)):
+def project(total, img_refs, picks, own_ref, peer_ref):
+    for slot, img_ref in zip(picks, img_refs):
         for j in range(0, N_SEC, 2):
             left = jnp.concatenate([img_ref[j], img_ref[j + 1]], axis=1)
             right = jnp.concatenate(
@@ -54,6 +53,15 @@
             )
             part = dot(left, right, NN)
             total = part if total is None else total + part
+    return total
+
+
+def project_early_kernel(a_ref, d_ref, own_ref, peer_ref, out_ref):
+    out_ref[...] = project(None, (a_ref, d_ref), (0, 3), own_ref, peer_ref)
+
+
+def project_kernel(part_ref, b_ref, c_ref, own_ref, peer_ref, out_ref, send_ref):
+    total = project(part_ref[...], (b_ref, c_ref), (1, 2), own_ref, peer_ref)
     out_ref[...] = total[:, : 2 * HD]
     send_ref[...] = total[:, 2 * HD :]
 
@@ -104,9 +112,13 @@
     grads_ref[...] = grads
 
 
-def join_kernel(keep_ref, a_ref, b_ref, c_ref, out_ref):
-    total = keep_ref[...] + a_ref[...].astype(F32)
-    total = (total + b_ref[...].astype(F32) + c_ref[...].astype(F32)).astype(BF16)
+def term_add_kernel(own_ref, peer_ref, grads_ref, others_ref, in_ref, out_ref):
+    grads = jnp.concatenate([grads_ref[...], others_ref[...]], axis=1)
+    out_ref[...] = term(own_ref, peer_ref, grads, 0) + in_ref[...].astype(F32)
+
+
+def join_kernel(keep_ref, b_ref, c_ref, out_ref):
+    total = (keep_ref[...] + b_ref[...].astype(F32) + c_ref[...].astype(F32)).astype(BF16)
     for j in range(N_SEC // 2):
         out_ref[j, 0] = total[j]
         out_ref[j, 1] = total[j + N_SEC // 2]
@@ -259,9 +271,10 @@
         load_kernel, (half, arr(BF16, *text.shape), arr(BF16, *upstream.shape)),
         [dma((2, N_HALF)), dma, dma], me, wk, wv, text, upstream,
     )
+    early = call(project_early_kernel, arr(F32, IMG, 4 * HD), 1 << 29, mine, img_opposite, own, peer)
+    img_first, img_second, early = lax.optimization_barrier((img_first, img_second, early))
     part, out_part = call(
-        project_kernel, (arr(F32, IMG, 2 * HD),) * 2, 1 << 30,
-        mine, img_first, img_second, img_opposite, own, peer,
+        project_kernel, (arr(F32, IMG, 2 * HD),) * 2, 1 << 29, early, img_first, img_second, own, peer
     )
     got_part = send(out_part, partner)
 
@@ -280,11 +293,13 @@
     got_opposite = send(terms(3, BF16), opposite)
     got_first = send(terms(1, BF16), first)
     got_second = send(terms(2, BF16), second)
-    keep = terms(0, F32)
+    keep = call(term_add_kernel, arr(F32, N_SEC, BLK, IMG), 1 << 28, own, peer, grads, others, got_opposite)
     attended = outside(attended_kernel, gates, probs, rows)
     d_query = outside(dquery_kernel, d_scores, rows)
-    keep, attended, d_query = lax.optimization_barrier((keep, attended, d_query))
-    total = call(join_kernel, arr(BF16, N_SEC // 2, 2, BLK, IMG), 1 << 20, keep, got_opposite, got_first, got_second)
+    got_first, got_second, keep, attended, d_query = lax.optimization_barrier(
+        (got_first, got_second, keep, attended, d_query)
+    )
+    total = call(join_kernel, arr(BF16, N_SEC // 2, 2, BLK, IMG), 1 << 20, keep, got_first, got_second)
     pieces = lax.all_to_all(total, "section", 0, 0, axis_index_groups=groups)
     stay, leave = call(
         half_kernel, (arr(F32, BLK, IMG), arr(BF16, BLK, IMG)), 1 << 20,

time: 102 us -> 102 us (level)
    pallas_call x8 -> x9, Pallas kernels: 4.66 us -> 4.79 us  [call(): pl.pallas_call(kernel, out_shape=outs, in_specs=[SMEM_SPEC if a.ndim == 1...]
  transfers between devices with their start and end apart: 11 -> 11, of which waited for: 7 -> 7; matrix products, arithmetic and copies ran while one was open for 0% -> 0% of each run, Pallas kernels for 5% -> 6%
where the time goes in v3:
time: 102 us; the launch traced here: 101 us
  starting transfers between devices  42.5 us (42%)
  blocking collectives  27.3 us (27%)
  waiting for transfers between devices  18.1 us (18%)
  Pallas kernels  10.7 us (10%)
  between operations  2.12 us (2%)
    ppermute x9, starting transfers between devices, send(): return lax.ppermute(x, 'tensor', perm)  30.6 us
    all_to_all x1, blocking collectives, shards(): lax.all_to_all(flat, 'section', 0, 0, axis_index_groups=groups)  14.8 us
    all_to_all x1, blocking collectives, shards(): pieces = lax.all_to_all(total, 'section', 0, 0, axis_index_groups=groups)  12.6 us
    ppermute x1, starting transfers between devices, shards(): passed = lax.ppermute(image, 'section', across)  9.1 us
    ppermute x9, waiting for transfers between devices, send(): return lax.ppermute(x, 'tensor', perm)  8.83 us
    ppermute x1, waiting for transfers between devices, shards(): lax.ppermute(leave, 'section', across).astype(F32)  7.2 us
    pallas_call x9, Pallas kernels, call(): pl.pallas_call(kernel, out_shape=outs, in_specs=[SMEM_SPEC if a.ndim == 1...  4.79 us
    pallas_call x2, Pallas kernels, load(): pl.pallas_call(kernel, out_shape=outs, in_specs=[SMEM_SPEC] + [pl.BlockSp...  3.52 us
  transfers between devices with their start and end apart: 11, of which 7 were waited for; matrix products, arithmetic and copies ran while one was open for 0% of the time, Pallas kernels for 6%

profile of v3, /device:TPU:24, one launch (start us, length us, event | category | flops | bytes accessed | tf_op | source)
XLA Modules:
  0.0 101.3 jit_solution(15088162006372136310)
XLA Ops:
  0.6 1.6 %shard_map.94 = bf16[2,4,8,128,128]{4,3,2,1,0:T(8,128)(2,1)S(1)} custom-call(s32[1]{0:T(128)} %bitcast.t_ref, bf16[8,8,128,128]{3,2,1,0:T(8,128)(2,1)} %bitcast.13, bf16[8,8,128,128]{3,2,1,0:T(8,128)(2,1)} %bitcast.15), custom_call_target="tpu_custom_call" | custom-call | bytes 6291456 | tf_op jit(solution)/shard_map/pallas_call | solution.py:217
  2.2 1.9 %collective-permute-start.1 = (bf16[2,4,8,128,128]{4,3,2,1,0:T(8,128)(2,1)S(1)}, bf16[2,4,8,128,128]{4,3,2,1,0:T(8,128)(2,1)S(1)}, u32[]{:S(2)}, u32[]{:S(2)}) collective-permute-start(bf16[2,4,8,128,128]{4,3,2,1,0:T(8,128)(2,1)S(1)} %shard_map.94), channel_id=1, source_target_pairs={{0,1},{1,0},{2,3},{3,2},{4,5},{5,4},{6,7},{7,6},{8,9},{9,8},{10,11... | collective-permute-start | bytes 6291464 | tf_op jit(solution)/shard_map/ppermute | solution.py:247
  4.2 9.1 %collective-permute-start = (bf16[128,128]{1,0:T(8,128)(2,1)S(1)}, bf16[128,128]{1,0:T(8,128)(2,1)S(1)}, u32[]{:S(2)}, u32[]{:S(2)}) collective-permute-start(bf16[128,128]{1,0:T(8,128)(2,1)S(1)} %copy-done), channel_id=1, source_target_pairs={{0,512},{128,640},{256,768},{384,896},{512,0},{640,128},{768,256},... | collective-permute-start | bytes 98312 | tf_op jit(solution)/shard_map/ppermute | solution.py:253
  13.3 2.0 %collective-permute-done.passed_ref = bf16[128,128]{1,0:T(8,128)(2,1)S(1)} collective-permute-done((bf16[128,128]{1,0:T(8,128)(2,1)S(1)}, bf16[128,128]{1,0:T(8,128)(2,1)S(1)}, u32[]{:S(2)}, u32[]{:S(2)}) %collective-permute-start) | collective-permute-done | bytes 32800 | tf_op jit(solution)/shard_map/ppermute | solution.py:253
  15.4 14.8 %all_to_all.10 = bf16[4,2,128,128]{3,2,1,0:T(8,128)(2,1)S(1)} all-to-all(bf16[4,2,128,128]{3,2,1,0:T(8,128)(2,1)S(1)} %pair.1), channel_id=1, replica_groups={{0,128,256,384},{512,640,768,896},{1,129,257,385},{513,641,769,897},{2,..., dimensions={0} | all-to-all | bytes 524288 | tf_op jit(solution)/shard_map/all_to_all | solution.py:265
  30.2 3.1 %collective-permute-start.4 = (bf16[8,128,128]{2,1,0:T(8,128)(2,1)S(1)}, bf16[8,128,128]{2,1,0:T(8,128)(2,1)S(1)}, u32[]{:S(2)}, u32[]{:S(2)}) collective-permute-start(bf16[8,128,128]{2,1,0:T(8,128)(2,1)S(1)} %bitcast.9), channel_id=1, source_target_pairs={{0,4},{1,5},{2,6},{3,7},{4,0},{5,1},{6,2},{7,3},{8,12},{9,13},{10,... | collective-permute-start | bytes 786440 | tf_op jit(solution)/shard_map/ppermute | solution.py:247
  33.3 8.4 %collective-permute-start.3 = (bf16[8,128,128]{2,1,0:T(8,128)(2,1)S(1)}, bf16[8,128,128]{2,1,0:T(8,128)(2,1)S(1)}, u32[]{:S(2)}, u32[]{:S(2)}) collective-permute-start(bf16[8,128,128]{2,1,0:T(8,128)(2,1)S(1)} %bitcast.10), channel_id=1, source_target_pairs={{0,6},{1,3},{2,4},{3,1},{4,2},{5,7},{6,0},{7,5},{8,14},{9,11},{10,... | collective-permute-start | bytes 786440 | tf_op jit(solution)/shard_map/ppermute | solution.py:247
  41.7 2.8 %collective-permute-start.2 = (bf16[8,128,128]{2,1,0:T(8,128)(2,1)S(1)}, bf16[8,128,128]{2,1,0:T(8,128)(2,1)S(1)}, u32[]{:S(2)}, u32[]{:S(2)}) collective-permute-start(bf16[8,128,128]{2,1,0:T(8,128)(2,1)S(1)} %bitcast.11), channel_id=1, source_target_pairs={{0,2},{1,7},{2,0},{3,5},{4,6},{5,3},{6,4},{7,1},{8,10},{9,15},{10,... | collective-permute-start | bytes 786440 | tf_op jit(solution)/shard_map/ppermute | solution.py:247
  44.5 1.9 %shard_map.95 = (bf16[2,4,8,128,128]{4,3,2,1,0:T(8,128)(2,1)S(1)}, bf16[256,1024]{1,0:T(8,128)(2,1)S(1)}, bf16[256,1024]{1,0:T(8,128)(2,1)S(1)}) custom-call(s32[1]{0:T(128)} %bitcast.t_ref, bf16[8,8,128,128]{3,2,1,0:T(8,128)(2,1)} %bitcast.14, bf16[8,8,128,128]{3,2,1,0:T(8,128)(2,1)} %bitcast.16, bf16[256,1024]{1,0:T(8,128)(2,1)} %bitcast.19, ...), custom_call_target="tpu_custom_call" | custom-call | bytes 6291456 | tf_op jit(solution)/shard_map/pallas_call | solution.py:217
  46.5 0.4 shard_map.96.part_ref
  46.9 2.8 %collective-permute-done.3.c_ref = bf16[8,128,128]{2,1,0:T(8,128)(2,1)S(1)} collective-permute-done((bf16[8,128,128]{2,1,0:T(8,128)(2,1)S(1)}, bf16[8,128,128]{2,1,0:T(8,128)(2,1)S(1)}, u32[]{:S(2)}, u32[]{:S(2)}) %collective-permute-start.3) | collective-permute-done | bytes 262176 | tf_op jit(solution)/shard_map/ppermute | solution.py:247
  49.8 0.2 collective-permute-done.2.b_ref
  50.0 0.5 shard_map.97
  50.5 1.9 %collective-permute-start.5 = (f32[128,256]{1,0:T(8,128)S(1)}, f32[128,256]{1,0:T(8,128)S(1)}, u32[]{:S(2)}, u32[]{:S(2)}) collective-permute-start(f32[128,256]{1,0:T(8,128)S(1)} %get-tuple-element.49), channel_id=1, source_target_pairs={{0,1},{1,0},{2,3},{3,2},{4,5},{5,4},{6,7},{7,6},{8,9},{9,8},{10,11... | collective-permute-start | bytes 393224 | tf_op jit(solution)/shard_map/ppermute | solution.py:247
  53.7 2.0 %shard_map.98 = (bf16[8,128,256]{2,1,0:T(8,128)(2,1)S(1)}, bf16[8,128,256]{2,1,0:T(8,128)(2,1)S(1)}, bf16[128,256]{1,0:T(8,128)(2,1)S(1)}, bf16[128,256]{1,0:T(8,128)(2,1)S(1)}) custom-call(s32[1]{0:T(128)S(6)} %copy.11.tiles_ref, f32[1]{0:T(128)S(6)} %copy.10.gate_ref, f32[128,256]{1,0:T(8,128)S(1)} %get-tuple-element.48.part_ref, ...), custom_call_target="tpu_custom_call" | custom-call | flops 1073741824 | bytes 1048576 | tf_op jit(solution)/shard_map/pallas_call | solution.py:170
  55.7 2.4 %collective-permute-start.6 = (bf16[128,256]{1,0:T(8,128)(2,1)S(1)}, bf16[128,256]{1,0:T(8,128)(2,1)S(1)}, u32[]{:S(2)}, u32[]{:S(2)}) collective-permute-start(bf16[128,256]{1,0:T(8,128)(2,1)S(1)} %get-tuple-element.52.grads_ref), channel_id=1, source_target_pairs={{0,1},{1,0},{2,3},{3,2},{4,5},{5,4},{6,7},{7,6},{8,9},{9,8},{10,11... | collective-permute-start | bytes 196616 | tf_op jit(solution)/shard_map/ppermute | solution.py:247
  58.1 0.9 collective-permute-done.6.others_ref
  59.0 0.4 shard_map.101
  59.5 4.8 %collective-permute-start.9 = (bf16[8,128,128]{2,1,0:T(8,128)(2,1)S(1)}, bf16[8,128,128]{2,1,0:T(8,128)(2,1)S(1)}, u32[]{:S(2)}, u32[]{:S(2)}) collective-permute-start(bf16[8,128,128]{2,1,0:T(8,128)(2,1)S(1)} %shard_map.101), channel_id=1, source_target_pairs={{0,4},{1,5},{2,6},{3,7},{4,0},{5,1},{6,2},{7,3},{8,12},{9,13},{10,... | collective-permute-start | bytes 786440 | tf_op jit(solution)/shard_map/ppermute | solution.py:247
  64.3 0.4 shard_map.99
  64.7 3.3 %collective-permute-start.7 = (bf16[8,128,128]{2,1,0:T(8,128)(2,1)S(1)}, bf16[8,128,128]{2,1,0:T(8,128)(2,1)S(1)}, u32[]{:S(2)}, u32[]{:S(2)}) collective-permute-start(bf16[8,128,128]{2,1,0:T(8,128)(2,1)S(1)} %shard_map.99), channel_id=1, source_target_pairs={{0,2},{1,7},{2,0},{3,5},{4,6},{5,3},{6,4},{7,1},{8,10},{9,15},{10,... | collective-permute-start | bytes 786440 | tf_op jit(solution)/shard_map/ppermute | solution.py:247
  68.0 0.4 shard_map.100
  68.5 1.9 %collective-permute-start.8 = (bf16[8,128,128]{2,1,0:T(8,128)(2,1)S(1)}, bf16[8,128,128]{2,1,0:T(8,128)(2,1)S(1)}, u32[]{:S(2)}, u32[]{:S(2)}) collective-permute-start(bf16[8,128,128]{2,1,0:T(8,128)(2,1)S(1)} %shard_map.100), channel_id=1, source_target_pairs={{0,6},{1,3},{2,4},{3,1},{4,2},{5,7},{6,0},{7,5},{8,14},{9,11},{10,... | collective-permute-start | bytes 786440 | tf_op jit(solution)/shard_map/ppermute | solution.py:247
  70.4 1.1 %shard_map.103 = bf16[256,1024]{1,0:T(8,128)(2,1)} custom-call(f32[1]{0:T(128)S(6)} %copy.10.gate_ref, bf16[8,128,256]{2,1,0:T(8,128)(2,1)S(1)} %get-tuple-element.53.probs_ref, bf16[128,256]{1,0:T(8,128)(2,1)S(1)} %get-tuple-element.54.rows_ref), custom_call_target="tpu_custom_call" | custom-call | flops 134217728 | bytes 1048576 | tf_op jit(solution)/shard_map/pallas_call | solution.py:181
  71.5 1.1 %shard_map.104 = bf16[256,1024]{1,0:T(8,128)(2,1)} custom-call(bf16[8,128,256]{2,1,0:T(8,128)(2,1)S(1)} %get-tuple-element.55.dscores_ref, bf16[128,256]{1,0:T(8,128)(2,1)S(1)} %get-tuple-element.54.rows_ref), custom_call_target="tpu_custom_call" | custom-call | flops 134217728 | bytes 1048576 | tf_op jit(solution)/shard_map/pallas_call | solution.py:181
  72.7 0.4 shard_map.102.keep_ref
  73.1 4.4 %collective-permute-done.7.b_ref = bf16[8,128,128]{2,1,0:T(8,128)(2,1)S(1)} collective-permute-done((bf16[8,128,128]{2,1,0:T(8,128)(2,1)S(1)}, bf16[8,128,128]{2,1,0:T(8,128)(2,1)S(1)}, u32[]{:S(2)}, u32[]{:S(2)}) %collective-permute-start.7) | collective-permute-done | bytes 262176 | tf_op jit(solution)/shard_map/ppermute | solution.py:247
  77.5 0.5 collective-permute-done.8.c_ref
  78.0 12.6 %all_to_all.11.in_ref = bf16[4,2,128,128]{3,2,1,0:T(8,128)(2,1)S(1)} all-to-all(bf16[4,2,128,128]{3,2,1,0:T(8,128)(2,1)S(1)} %shard_map.105), channel_id=1, replica_groups={{0,128,256,384},{512,640,768,896},{1,129,257,385},{513,641,769,897},{2,..., dimensions={0} | all-to-all | bytes 524288 | tf_op jit(solution)/shard_map/all_to_all | solution.py:303
  90.7 2.9 %collective-permute-start.10 = (bf16[128,128]{1,0:T(8,128)(2,1)S(1)}, bf16[128,128]{1,0:T(8,128)(2,1)S(1)}, u32[]{:S(2)}, u32[]{:S(2)}) collective-permute-start(bf16[128,128]{1,0:T(8,128)(2,1)S(1)} %get-tuple-element.62), channel_id=1, source_target_pairs={{0,512},{128,640},{256,768},{384,896},{512,0},{640,128},{768,256},... | collective-permute-start | bytes 98312 | tf_op jit(solution)/shard_map/ppermute | solution.py:308
  93.5 7.2 %collective-permute-done.10 = bf16[128,128]{1,0:T(8,128)(2,1)S(1)} collective-permute-done((bf16[128,128]{1,0:T(8,128)(2,1)S(1)}, bf16[128,128]{1,0:T(8,128)(2,1)S(1)}, u32[]{:S(2)}, u32[]{:S(2)}) %collective-permute-start.10) | collective-permute-done | bytes 32800 | tf_op jit(solution)/shard_map/ppermute | solution.py:308
  100.7 0.6 add_convert_fusion
  (9 shorter events, 0.3 us)
Async XLA Ops:
  0.6 3.5 %copy-start = (bf16[128,128]{1,0:T(8,128)(2,1)S(1)}, bf16[128,128]{1,0:T(8,128)(2,1)}, u32[]{:S(2)}) copy-start(bf16[128,128]{1,0:T(8,128)(2,1)} %own_ref) | copy-start | bytes 98308
  2.2 44.2 %collective-permute-start.1 = (bf16[2,4,8,128,128]{4,3,2,1,0:T(8,128)(2,1)S(1)}, bf16[2,4,8,128,128]{4,3,2,1,0:T(8,128)(2,1)S(1)}, u32[]{:S(2)}, u32[]{:S(2)}) collective-permute-start(bf16[2,4,8,128,128]{4,3,2,1,0:T(8,128)(2,1)S(1)} %shard_map.94), channel_id=1, source_target_pairs={{0,1},{1,0},{2,3},{3,2},{4,5},{5,4},{6,7},{7,6},{8,9},{9,8},{10,11... | collective-permute-start | bytes 6291464 | tf_op jit(solution)/shard_map/ppermute | solution.py:247
  4.2 11.1 %collective-permute-start = (bf16[128,128]{1,0:T(8,128)(2,1)S(1)}, bf16[128,128]{1,0:T(8,128)(2,1)S(1)}, u32[]{:S(2)}, u32[]{:S(2)}) collective-permute-start(bf16[128,128]{1,0:T(8,128)(2,1)S(1)} %copy-done), channel_id=1, source_target_pairs={{0,512},{128,640},{256,768},{384,896},{512,0},{640,128},{768,256},... | collective-permute-start | bytes 98312 | tf_op jit(solution)/shard_map/ppermute | solution.py:253
  30.2 16.3 %collective-permute-start.4 = (bf16[8,128,128]{2,1,0:T(8,128)(2,1)S(1)}, bf16[8,128,128]{2,1,0:T(8,128)(2,1)S(1)}, u32[]{:S(2)}, u32[]{:S(2)}) collective-permute-start(bf16[8,128,128]{2,1,0:T(8,128)(2,1)S(1)} %bitcast.9), channel_id=1, source_target_pairs={{0,4},{1,5},{2,6},{3,7},{4,0},{5,1},{6,2},{7,3},{8,12},{9,13},{10,... | collective-permute-start | bytes 786440 | tf_op jit(solution)/shard_map/ppermute | solution.py:247
  33.3 16.4 %collective-permute-start.3 = (bf16[8,128,128]{2,1,0:T(8,128)(2,1)S(1)}, bf16[8,128,128]{2,1,0:T(8,128)(2,1)S(1)}, u32[]{:S(2)}, u32[]{:S(2)}) collective-permute-start(bf16[8,128,128]{2,1,0:T(8,128)(2,1)S(1)} %bitcast.10), channel_id=1, source_target_pairs={{0,6},{1,3},{2,4},{3,1},{4,2},{5,7},{6,0},{7,5},{8,14},{9,11},{10,... | collective-permute-start | bytes 786440 | tf_op jit(solution)/shard_map/ppermute | solution.py:247
  41.7 8.3 %collective-permute-start.2 = (bf16[8,128,128]{2,1,0:T(8,128)(2,1)S(1)}, bf16[8,128,128]{2,1,0:T(8,128)(2,1)S(1)}, u32[]{:S(2)}, u32[]{:S(2)}) collective-permute-start(bf16[8,128,128]{2,1,0:T(8,128)(2,1)S(1)} %bitcast.11), channel_id=1, source_target_pairs={{0,2},{1,7},{2,0},{3,5},{4,6},{5,3},{6,4},{7,1},{8,10},{9,15},{10,... | collective-permute-start | bytes 786440 | tf_op jit(solution)/shard_map/ppermute | solution.py:247
  50.5 3.2 %collective-permute-start.5 = (f32[128,256]{1,0:T(8,128)S(1)}, f32[128,256]{1,0:T(8,128)S(1)}, u32[]{:S(2)}, u32[]{:S(2)}) collective-permute-start(f32[128,256]{1,0:T(8,128)S(1)} %get-tuple-element.49), channel_id=1, source_target_pairs={{0,1},{1,0},{2,3},{3,2},{4,5},{5,4},{6,7},{7,6},{8,9},{9,8},{10,11... | collective-permute-start | bytes 393224 | tf_op jit(solution)/shard_map/ppermute | solution.py:247
  55.7 3.3 %collective-permute-start.6 = (bf16[128,256]{1,0:T(8,128)(2,1)S(1)}, bf16[128,256]{1,0:T(8,128)(2,1)S(1)}, u32[]{:S(2)}, u32[]{:S(2)}) collective-permute-start(bf16[128,256]{1,0:T(8,128)(2,1)S(1)} %get-tuple-element.52.grads_ref), channel_id=1, source_target_pairs={{0,1},{1,0},{2,3},{3,2},{4,5},{5,4},{6,7},{7,6},{8,9},{9,8},{10,11... | collective-permute-start | bytes 196616 | tf_op jit(solution)/shard_map/ppermute | solution.py:247
  59.5 13.2 %collective-permute-start.9 = (bf16[8,128,128]{2,1,0:T(8,128)(2,1)S(1)}, bf16[8,128,128]{2,1,0:T(8,128)(2,1)S(1)}, u32[]{:S(2)}, u32[]{:S(2)}) collective-permute-start(bf16[8,128,128]{2,1,0:T(8,128)(2,1)S(1)} %shard_map.101), channel_id=1, source_target_pairs={{0,4},{1,5},{2,6},{3,7},{4,0},{5,1},{6,2},{7,3},{8,12},{9,13},{10,... | collective-permute-start | bytes 786440 | tf_op jit(solution)/shard_map/ppermute | solution.py:247
  64.7 12.7 %collective-permute-start.7 = (bf16[8,128,128]{2,1,0:T(8,128)(2,1)S(1)}, bf16[8,128,128]{2,1,0:T(8,128)(2,1)S(1)}, u32[]{:S(2)}, u32[]{:S(2)}) collective-permute-start(bf16[8,128,128]{2,1,0:T(8,128)(2,1)S(1)} %shard_map.99), channel_id=1, source_target_pairs={{0,2},{1,7},{2,0},{3,5},{4,6},{5,3},{6,4},{7,1},{8,10},{9,15},{10,... | collective-permute-start | bytes 786440 | tf_op jit(solution)/shard_map/ppermute | solution.py:247
  68.5 9.5 %collective-permute-start.8 = (bf16[8,128,128]{2,1,0:T(8,128)(2,1)S(1)}, bf16[8,128,128]{2,1,0:T(8,128)(2,1)S(1)}, u32[]{:S(2)}, u32[]{:S(2)}) collective-permute-start(bf16[8,128,128]{2,1,0:T(8,128)(2,1)S(1)} %shard_map.100), channel_id=1, source_target_pairs={{0,6},{1,3},{2,4},{3,1},{4,2},{5,7},{6,0},{7,5},{8,14},{9,11},{10,... | collective-permute-start | bytes 786440 | tf_op jit(solution)/shard_map/ppermute | solution.py:247
  90.7 10.1 %collective-permute-start.10 = (bf16[128,128]{1,0:T(8,128)(2,1)S(1)}, bf16[128,128]{1,0:T(8,128)(2,1)S(1)}, u32[]{:S(2)}, u32[]{:S(2)}) collective-permute-start(bf16[128,128]{1,0:T(8,128)(2,1)S(1)} %get-tuple-element.62), channel_id=1, source_target_pairs={{0,512},{128,640},{256,768},{384,896},{512,0},{640,128},{768,256},... | collective-permute-start | bytes 98312 | tf_op jit(solution)/shard_map/ppermute | solution.py:308
